TPU v7x, 32 devices: a whole 2x2x4 slice. The times are simulated.
32 devices in a mesh: sec: 4 (over x, core), row: 4 (over z), col: 2 (over y).
Axes of the slice: x: 2, y: 2, z: 4, core: 2. Of those that a mesh axis runs over, the one named last changes fastest.
Arguments:
- images: float32 [4, 1024, 512], P('sec', 'row', 'col'), may hold values from -6 to 6
- stiffness: float32 [4, 1024, 512], P('sec', 'row', 'col'), may hold values from 0.1 to 1
Outputs:
- tensor: float32 [5, 4, 1024, 512], P(None, 'sec', 'row', 'col')
- field: float32 [2, 4, 1024, 512], P(None, 'sec', 'row', 'col')
All inputs are finite; a program needn't handle non-finite values.
Results may differ from a plain program's by a relative error of at most 0.00002.
Values sent between devices are 32-bit elements; how exact they have to be, the bound alone decides.
A program may use at most 64 MiB of HBM per device.

v0:
```python
import jax
import jax.numpy as jnp
from jax import lax
from jax.sharding import PartitionSpec as P

RADIUS = 4
SWEEPS = 4
ROUNDS = 2


coupling = 0.25


def from_behind(value, axis, steps):
    count = lax.axis_size(axis)
    first, last = (max(0, -steps), min(count, count - steps))
    return lax.ppermute(value, axis, [(source, source + steps) for source in range(first, last)])


def extended(x, sides, width):
    for axis, dim in sides:
        size, length = (lax.axis_size(axis), x.shape[dim])
        up = [(i, (i + 1) % size) for i in range(size - 1)]
        down = [(j, i) for i, j in up]
        last = lax.slice_in_dim(x, length - width, length, axis=dim)
        first = lax.slice_in_dim(x, 0, width, axis=dim)
        before = lax.ppermute(last, axis, up)
        after = lax.ppermute(first, axis, down)
        x = jnp.concatenate([before, x, after], axis=dim)
    return x


def gradients(padded):
    grad_y = (padded[..., 2:, 1:-1] - padded[..., :-2, 1:-1]) * 0.5
    grad_x = (padded[..., 1:-1, 2:] - padded[..., 1:-1, :-2]) * 0.5
    return (grad_y, grad_x)


def products(grad_y, grad_x, change):
    return jnp.stack(
        [grad_x * grad_x, grad_x * grad_y, grad_y * grad_y, grad_x * change, grad_y * change]
    )


def window_mean(widened, radius):
    row_count = widened.shape[-2] - 2 * radius
    col_count = widened.shape[-1] - 2 * radius
    partial_rows = widened[..., 0:row_count, :]
    for offset in range(1, 2 * radius + 1):
        partial_rows = partial_rows + widened[..., offset : offset + row_count, :]
    summed = partial_rows[..., 0:col_count]
    for offset in range(1, 2 * radius + 1):
        summed = summed + partial_rows[..., offset : offset + col_count]
    return summed / float((2 * radius + 1) ** 2)


def couplings(stiff_pad):
    centre = stiff_pad[..., 1:-1, 1:-1]
    kappa_up = jnp.sqrt(centre * stiff_pad[..., :-2, 1:-1])
    kappa_down = jnp.sqrt(centre * stiff_pad[..., 2:, 1:-1])
    kappa_left = jnp.sqrt(centre * stiff_pad[..., 1:-1, :-2])
    kappa_right = jnp.sqrt(centre * stiff_pad[..., 1:-1, 2:])
    kappa_sum = kappa_up + kappa_down + kappa_left + kappa_right
    return ((kappa_up, kappa_down, kappa_left, kappa_right), kappa_sum)


def jacobi(field_pad, kappas, kappa_sum, tensor, beside):
    neighbour = kappas[0] * field_pad[..., :-2, 1:-1] + kappas[1] * field_pad[..., 2:, 1:-1]
    neighbour = (
        neighbour + kappas[2] * field_pad[..., 1:-1, :-2] + kappas[3] * field_pad[..., 1:-1, 2:]
    )
    diagonal = kappa_sum + 2.0 * coupling
    first_diag = tensor[0] + diagonal
    second_diag = tensor[2] + diagonal
    off_diag = tensor[1]
    determinant = first_diag * second_diag - off_diag * off_diag
    right_x = coupling * beside[0] + neighbour[0] - tensor[3]
    right_y = coupling * beside[1] + neighbour[1] - tensor[4]
    new_x = (second_diag * right_x - off_diag * right_y) / determinant
    new_y = (first_diag * right_y - off_diag * right_x) / determinant
    return jnp.stack([new_x, new_y])


def trimmed(values, margin):
    if margin == 0:
        return values
    return values[..., margin : values.shape[-2] - margin, margin : values.shape[-1] - margin]


def neighbours(field, round_index):
    if round_index == 0:
        return jnp.zeros_like(field)
    before = from_behind(field, "sec", 1)
    after = from_behind(field, "sec", -1)
    below_part = jnp.concatenate([before, field[:, :-1]], axis=1)
    above_part = jnp.concatenate([field[:, 1:], after], axis=1)
    return below_part + above_part


def local(images, stiffness):
    local_count = images.shape[0]
    earlier = from_behind(images, "sec", 1)
    first = jnp.concatenate([earlier, images[: local_count - 1]], axis=0)
    rimmed = extended(first, (("row", 1), ("col", 2)), 1)
    grad_y, grad_x = gradients(rimmed)
    stacked = products(grad_y, grad_x, images - first)
    widened = extended(stacked, (("row", 2), ("col", 3)), RADIUS)
    tensor = window_mean(widened, RADIUS)
    returned = from_behind(tensor, "sec", -1)
    tensor = jnp.concatenate([tensor[:, 1:], returned], axis=1)
    field = jnp.zeros((2,) + images.shape, jnp.float32)
    stiff_rims = extended(stiffness, (("row", 1), ("col", 2)), SWEEPS)
    kappas_wide, sum_wide = couplings(stiff_rims)
    tensor_wide = extended(tensor, (("row", 2), ("col", 3)), SWEEPS - 1)
    for round_index in range(ROUNDS):
        beside = neighbours(field, round_index)
        joined = extended(
            jnp.concatenate([field, beside], axis=0), (("row", 2), ("col", 3)), SWEEPS
        )
        moving = joined[0:2]
        for sweep_index in range(SWEEPS):
            kappas_now = tuple((trimmed(kappa_part, sweep_index) for kappa_part in kappas_wide))
            moving = jacobi(
                moving,
                kappas_now,
                trimmed(sum_wide, sweep_index),
                trimmed(tensor_wide, sweep_index),
                trimmed(joined[2:4], sweep_index + 1),
            )
        field = moving
    return (tensor, field)


def solution(mesh):
    in_specs = (P("sec", "row", "col"), P("sec", "row", "col"))
    out_specs = (P(None, "sec", "row", "col"), P(None, "sec", "row", "col"))
    return jax.shard_map(local, mesh=mesh, in_specs=in_specs, out_specs=out_specs, check_vma=False)
```

profile of v0, /device:TPU:1, one launch (start us, length us, event | category | flops | bytes accessed | tf_op | source)
XLA Modules:
  0.0 177.0 jit_solution(6112393179807467891)
XLA Ops:
  1.4 4.0 %collective-permute-start.10 = (f32[1,4,256]{2,1,0:T(4,128)S(1)}, f32[1,4,256]{2,1,0:T(4,128)S(1)}, u32[]{:S(2)}, u32[]{:S(2)}) collective-permute-start(f32[1,4,256]{2,1,0:T(4,128)S(1)} %get-tuple-element.43), channel_id=1, source_target_pairs={{0,2},{2,4},{4,6},{1,3},{3,5},{5,7},{8,10},{10,12},{12,14},{9,11},... | collective-permute-start | bytes 12296 | tf_op jit(solution)/shard_map/ppermute | solution.py:27
  6.7 4.0 %collective-permute-start.18 = (f32[4,1,4,256]{3,2,1,0:T(4,128)S(1)}, f32[4,1,4,256]{3,2,1,0:T(4,128)S(1)}, u32[]{:S(2)}, u32[]{:S(2)}) collective-permute-start(f32[4,1,4,256]{3,2,1,0:T(4,128)S(1)} %broadcast.259), channel_id=1, source_target_pairs={{0,2},{2,4},{4,6},{1,3},{3,5},{5,7},{8,10},{10,12},{12,14},{9,11},... | collective-permute-start | bytes 49160 | tf_op jit(solution)/shard_map/ppermute | solution.py:27
  12.0 4.5 %collective-permute-start = (f32[1,256,256]{2,1,0:T(8,128)}, f32[1,256,256]{2,1,0:T(8,128)S(1)}, u32[]{:S(2)}, u32[]{:S(2)}) collective-permute-start(f32[1,256,256]{2,1,0:T(8,128)} %param.2), channel_id=1, source_target_pairs={{0,8},{8,16},{16,24},{1,9},{9,17},{17,25},{2,10},{10,18},{18,26},{... | collective-permute-start | bytes 786440 | tf_op jit(solution)/shard_map/ppermute | solution.py:17
  17.6 3.2 %collective-permute-start.12 = (f32[1,264,4]{2,1,0:T(8,128)S(1)}, f32[1,264,4]{2,1,0:T(8,128)S(1)}, u32[]{:S(2)}, u32[]{:S(2)}) collective-permute-start(f32[1,264,4]{2,1,0:T(8,128)S(1)} %get-tuple-element.39), channel_id=1, source_target_pairs={{0,1},{2,3},{4,5},{6,7},{8,9},{10,11},{12,13},{14,15},{16,17},{18,... | collective-permute-start | bytes 12680 | tf_op jit(solution)/shard_map/ppermute | solution.py:27
  22.1 4.3 %collective-permute-start.1 = (f32[1,1,256]{2,1,0:T(1,128)S(1)}, f32[1,1,256]{2,1,0:T(1,128)S(1)}, u32[]{:S(2)}, u32[]{:S(2)}) collective-permute-start(f32[1,1,256]{2,1,0:T(1,128)S(1)} %get-tuple-element.45), channel_id=1, source_target_pairs={{0,2},{2,4},{4,6},{1,3},{3,5},{5,7},{8,10},{10,12},{12,14},{9,11},... | collective-permute-start | bytes 3080 | tf_op jit(solution)/shard_map/ppermute | solution.py:27
  32.1 4.0 %collective-permute-start.4 = (f32[1,258,1]{2,1,0:T(8,128)S(1)}, f32[1,258,1]{2,1,0:T(8,128)S(1)}, u32[]{:S(2)}, u32[]{:S(2)}) collective-permute-start(f32[1,258,1]{2,1,0:T(8,128)S(1)} %get-tuple-element.42), channel_id=1, source_target_pairs={{0,1},{2,3},{4,5},{6,7},{8,9},{10,11},{12,13},{14,15},{16,17},{18,... | collective-permute-start | bytes 3104 | tf_op jit(solution)/shard_map/ppermute | solution.py:27
  39.7 3.2 %collective-permute-start.5 = (f32[5,1,4,256]{3,2,1,0:T(4,128)S(1)}, f32[5,1,4,256]{3,2,1,0:T(4,128)S(1)}, u32[]{:S(2)}, u32[]{:S(2)}) collective-permute-start(f32[5,1,4,256]{3,2,1,0:T(4,128)S(1)} %get-tuple-element.27), channel_id=1, source_target_pairs={{0,2},{2,4},{4,6},{1,3},{3,5},{5,7},{8,10},{10,12},{12,14},{9,11},... | collective-permute-start | bytes 61448 | tf_op jit(solution)/shard_map/ppermute | solution.py:27
  50.2 4.1 %collective-permute-start.7 = (f32[5,1,264,4]{2,3,1,0:T(4,128)S(1)}, f32[5,1,264,4]{2,3,1,0:T(4,128)S(1)}, u32[]{:S(2)}, u32[]{:S(2)}) collective-permute-start(f32[5,1,264,4]{2,3,1,0:T(4,128)S(1)} %copy.15), channel_id=1, source_target_pairs={{0,1},{2,3},{4,5},{6,7},{8,9},{10,11},{12,13},{14,15},{16,17},{18,... | collective-permute-start | bytes 63368 | tf_op jit(solution)/shard_map/ppermute | solution.py:27
  61.5 2.1 %pad_maximum_fusion = f32[5,1,264,264]{3,2,1,0:T(8,128)S(1)} fusion(f32[5,1,264,4]{3,2,1,0:T(8,128)} %copy.18, f32[5,1,4,256]{3,2,1,0:T(4,128)S(1)} %collective-permute-done.6, f32[5,1,256,256]{3,2,1,0:T(8,128)S(1)} %bitcast_dynamic-update-slice_fusion, f32[5,1,4,256]{3,2,1,0:T(4,128)S(1)} %collective-permute-done.5, f32[5,1,264,4]{3,2,1,0:T(8,128)} %copy.17), kind=kLoop, calls=%fused_computation | loop fusion | flops 1393920 | bytes 2787840 | tf_op jit(solution)/shard_map/concatenate | solution.py:29
  65.1 3.8 %fusion = f32[5,1,256,256]{3,2,1,0:T(8,128)} fusion(f32[5,1,256,264]{3,2,1,0:T(8,128)S(1)} %slice_add_fusion), kind=kLoop, calls=%fused_computation.15 | loop fusion | flops 2949120 | bytes 13107200 | tf_op jit(solution)/shard_map/div | solution.py:54
  68.9 5.9 %collective-permute-start.9 = (f32[5,1,256,256]{3,2,1,0:T(8,128)}, f32[5,1,256,256]{3,2,1,0:T(8,128)S(1)}, u32[]{:S(2)}, u32[]{:S(2)}) collective-permute-start(f32[5,1,256,256]{3,2,1,0:T(8,128)} %fusion), channel_id=1, source_target_pairs={{8,0},{16,8},{24,16},{9,1},{17,9},{25,17},{10,2},{18,10},{26,18},{... | collective-permute-start | bytes 3932168 | tf_op jit(solution)/shard_map/ppermute | solution.py:17
  81.8 2.1 %collective-permute-start.20 = (f32[4,1,264,4]{2,3,1,0:T(4,128)S(1)}, f32[4,1,264,4]{2,3,1,0:T(4,128)S(1)}, u32[]{:S(2)}, u32[]{:S(2)}) collective-permute-start(f32[4,1,264,4]{2,3,1,0:T(4,128)S(1)} %copy.27), channel_id=1, source_target_pairs={{0,1},{2,3},{4,5},{6,7},{8,9},{10,11},{12,13},{14,15},{16,17},{18,... | collective-permute-start | bytes 50696 | tf_op jit(solution)/shard_map/ppermute | solution.py:27
  91.5 3.2 %collective-permute-start.14 = (f32[5,1,3,256]{3,1,2,0:T(1,128)S(1)}, f32[5,1,3,256]{3,1,2,0:T(1,128)S(1)}, u32[]{:S(2)}, u32[]{:S(2)}) collective-permute-start(f32[5,1,3,256]{3,1,2,0:T(1,128)S(1)} %copy.19), channel_id=1, source_target_pairs={{0,2},{2,4},{4,6},{1,3},{3,5},{5,7},{8,10},{10,12},{12,14},{9,11},... | collective-permute-start | bytes 46088 | tf_op jit(solution)/shard_map/ppermute | solution.py:27
  96.2 2.2 %pad_maximum_fusion.2 = f32[4,1,264,264]{3,2,1,0:T(8,128)S(1)} fusion(f32[4,1,264,4]{3,2,1,0:T(8,128)} %copy.30, f32[4,1,4,256]{3,2,1,0:T(4,128)S(1)} %collective-permute-done.19, f32[4,1,256,256]{3,2,1,0:T(8,128)} %copy-done.17, f32[4,1,4,256]{3,2,1,0:T(4,128)S(1)} %collective-permute-done.18, f32[4,1,264,4]{3,2,1,0:T(8,128)} %copy.29), kind=kLoop, calls=%fused_computation.10 | loop fusion | flops 1115136 | bytes 2230272 | tf_op jit(solution)/shard_map/concatenate | solution.py:29
  102.2 2.4 %collective-permute-start.16 = (f32[5,1,262,3]{2,0,3,1:T(8,128)S(1)}, f32[5,1,262,3]{2,0,3,1:T(8,128)S(1)}, u32[]{:S(2)}, u32[]{:S(2)}) collective-permute-start(f32[5,1,262,3]{2,0,3,1:T(8,128)S(1)} %copy.23), channel_id=1, source_target_pairs={{0,1},{2,3},{4,5},{6,7},{8,9},{10,11},{12,13},{14,15},{16,17},{18,... | collective-permute-start | bytes 47168 | tf_op jit(solution)/shard_map/ppermute | solution.py:27
  107.5 2.9 %fusion.44 = f32[2,1,262,262]{3,2,1,0:T(8,128)} fusion(f32[4,1,264,264]{3,2,1,0:T(8,128)S(1)} %pad_maximum_fusion.2, f32[262,262]{1,0:T(8,128)} %bitcast.312, f32[262,262]{1,0:T(8,128)} %bitcast.308, f32[262,262]{1,0:T(8,128)} %bitcast.310, f32[262,262]{1,0:T(8,128)S(1)} %bitcast.306), kind=kLoop, calls=%fused_computation.113 | loop fusion | flops 961016 | bytes 3844064 | tf_op jit(solution)/shard_map/add | solution.py:70
  112.8 2.3 %pad_maximum_fusion.1 = f32[5,1,262,262]{3,2,1,0:T(8,128)S(1)} fusion(f32[5,1,262,3]{3,2,1,0:T(8,128)} %copy.26, f32[5,1,3,256]{3,2,1,0:T(4,128)S(1)} %copy.22, f32[5,1,256,256]{3,2,1,0:T(8,128)S(1)} %collective-permute-done.9, f32[5,1,3,256]{3,2,1,0:T(4,128)S(1)} %copy.21, f32[5,1,262,3]{3,2,1,0:T(8,128)} %copy.25), kind=kLoop, calls=%fused_computation.1 | loop fusion | flops 1372880 | bytes 2745760 | tf_op jit(solution)/shard_map/concatenate | solution.py:29
  126.4 4.7 %collective-permute-start.22 = (f32[2,1,256,256]{3,2,1,0:T(8,128)S(1)}, f32[2,1,256,256]{3,2,1,0:T(8,128)S(1)}, u32[]{:S(2)}, u32[]{:S(2)}) collective-permute-start(f32[2,1,256,256]{3,2,1,0:T(8,128)S(1)} %pad_maximum_fusion.14), channel_id=1, source_target_pairs={{0,8},{8,16},{16,24},{1,9},{9,17},{17,25},{2,10},{10,18},{18,26},{... | collective-permute-start | bytes 1572872 | tf_op jit(solution)/shard_map/ppermute | solution.py:17
  133.1 4.2 %collective-permute-done.22 = f32[2,1,256,256]{3,2,1,0:T(8,128)S(1)} collective-permute-done((f32[2,1,256,256]{3,2,1,0:T(8,128)S(1)}, f32[2,1,256,256]{3,2,1,0:T(8,128)S(1)}, u32[]{:S(2)}, u32[]{:S(2)}) %collective-permute-start.22) | collective-permute-done | bytes 524320 | tf_op jit(solution)/shard_map/ppermute | solution.py:17
  137.2 4.4 %collective-permute-done.23 = f32[2,1,256,256]{3,2,1,0:T(8,128)S(1)} collective-permute-done((f32[2,1,256,256]{3,2,1,0:T(8,128)S(1)}, f32[2,1,256,256]{3,2,1,0:T(8,128)S(1)}, u32[]{:S(2)}, u32[]{:S(2)}) %collective-permute-start.23) | collective-permute-done | bytes 524320 | tf_op jit(solution)/shard_map/ppermute | solution.py:17
  141.7 2.6 %collective-permute-start.24 = (f32[4,1,4,256]{3,2,1,0:T(4,128)S(1)}, f32[4,1,4,256]{3,2,1,0:T(4,128)S(1)}, u32[]{:S(2)}, u32[]{:S(2)}) collective-permute-start(f32[4,1,4,256]{3,2,1,0:T(4,128)S(1)} %get-tuple-element.33), channel_id=1, source_target_pairs={{0,2},{2,4},{4,6},{1,3},{3,5},{5,7},{8,10},{10,12},{12,14},{9,11},... | collective-permute-start | bytes 49160 | tf_op jit(solution)/shard_map/ppermute | solution.py:27
  145.6 3.2 %collective-permute-done.25 = f32[4,1,4,256]{3,2,1,0:T(4,128)S(1)} collective-permute-done((f32[4,1,4,256]{3,2,1,0:T(4,128)S(1)}, f32[4,1,4,256]{3,2,1,0:T(4,128)S(1)}, u32[]{:S(2)}, u32[]{:S(2)}) %collective-permute-start.25) | collective-permute-done | bytes 16416 | tf_op jit(solution)/shard_map/ppermute | solution.py:28
  151.4 4.4 %collective-permute-start.26 = (f32[4,1,264,4]{2,3,1,0:T(4,128)S(1)}, f32[4,1,264,4]{2,3,1,0:T(4,128)}, u32[]{:S(2)}, u32[]{:S(2)}) collective-permute-start(f32[4,1,264,4]{2,3,1,0:T(4,128)S(1)} %copy.31), channel_id=1, source_target_pairs={{0,1},{2,3},{4,5},{6,7},{8,9},{10,11},{12,13},{14,15},{16,17},{18,... | collective-permute-start | bytes 50696 | tf_op jit(solution)/shard_map/ppermute | solution.py:27
  164.6 2.0 %pad_maximum_fusion.3 = f32[4,1,264,264]{3,2,1,0:T(8,128)S(1)} fusion(f32[4,1,264,4]{3,2,1,0:T(8,128)} %copy.34, f32[4,1,4,256]{3,2,1,0:T(4,128)S(1)} %collective-permute-done.25, f32[2,1,256,256]{3,2,1,0:T(8,128)S(1)} %add.461, f32[1,1,256,256]{3,2,1,0:T(8,128)S(1)} %divide_bitcast_fusion.14, f32[1,1,256,256]{3,2,1,0:T(8,128)S(1)} %get-tuple-element.4, ...), kind=kLoop, calls=%fused_computation.11 | loop fusion | flops 1672704 | bytes 2230272 | tf_op jit(solution)/shard_map/concatenate | solution.py:29
  (218 shorter events, 91.7 us)
Async XLA Ops:
  1.4 15.2 %collective-permute-start.10 = (f32[1,4,256]{2,1,0:T(4,128)S(1)}, f32[1,4,256]{2,1,0:T(4,128)S(1)}, u32[]{:S(2)}, u32[]{:S(2)}) collective-permute-start(f32[1,4,256]{2,1,0:T(4,128)S(1)} %get-tuple-element.43), channel_id=1, source_target_pairs={{0,2},{2,4},{4,6},{1,3},{3,5},{5,7},{8,10},{10,12},{12,14},{9,11},... | collective-permute-start | bytes 12296 | tf_op jit(solution)/shard_map/ppermute | solution.py:27
  5.4 11.2 %collective-permute-start.11 = (f32[1,4,256]{2,1,0:T(4,128)S(1)}, f32[1,4,256]{2,1,0:T(4,128)S(1)}, u32[]{:S(2)}, u32[]{:S(2)}) collective-permute-start(f32[1,4,256]{2,1,0:T(4,128)S(1)} %get-tuple-element.44), channel_id=1, source_target_pairs={{2,0},{4,2},{6,4},{3,1},{5,3},{7,5},{10,8},{12,10},{14,12},{11,9},... | collective-permute-start | bytes 12296 | tf_op jit(solution)/shard_map/ppermute | solution.py:28
  6.7 71.6 %collective-permute-start.18 = (f32[4,1,4,256]{3,2,1,0:T(4,128)S(1)}, f32[4,1,4,256]{3,2,1,0:T(4,128)S(1)}, u32[]{:S(2)}, u32[]{:S(2)}) collective-permute-start(f32[4,1,4,256]{3,2,1,0:T(4,128)S(1)} %broadcast.259), channel_id=1, source_target_pairs={{0,2},{2,4},{4,6},{1,3},{3,5},{5,7},{8,10},{10,12},{12,14},{9,11},... | collective-permute-start | bytes 49160 | tf_op jit(solution)/shard_map/ppermute | solution.py:27
  10.7 67.6 %collective-permute-start.19 = (f32[4,1,4,256]{3,2,1,0:T(4,128)S(1)}, f32[4,1,4,256]{3,2,1,0:T(4,128)S(1)}, u32[]{:S(2)}, u32[]{:S(2)}) collective-permute-start(f32[4,1,4,256]{3,2,1,0:T(4,128)S(1)} %broadcast.259), channel_id=1, source_target_pairs={{2,0},{4,2},{6,4},{3,1},{5,3},{7,5},{10,8},{12,10},{14,12},{11,9},... | collective-permute-start | bytes 49160 | tf_op jit(solution)/shard_map/ppermute | solution.py:28
  12.0 10.1 %collective-permute-start = (f32[1,256,256]{2,1,0:T(8,128)}, f32[1,256,256]{2,1,0:T(8,128)S(1)}, u32[]{:S(2)}, u32[]{:S(2)}) collective-permute-start(f32[1,256,256]{2,1,0:T(8,128)} %param.2), channel_id=1, source_target_pairs={{0,8},{8,16},{16,24},{1,9},{9,17},{17,25},{2,10},{10,18},{18,26},{... | collective-permute-start | bytes 786440 | tf_op jit(solution)/shard_map/ppermute | solution.py:17
  17.6 8.8 %collective-permute-start.12 = (f32[1,264,4]{2,1,0:T(8,128)S(1)}, f32[1,264,4]{2,1,0:T(8,128)S(1)}, u32[]{:S(2)}, u32[]{:S(2)}) collective-permute-start(f32[1,264,4]{2,1,0:T(8,128)S(1)} %get-tuple-element.39), channel_id=1, source_target_pairs={{0,1},{2,3},{4,5},{6,7},{8,9},{10,11},{12,13},{14,15},{16,17},{18,... | collective-permute-start | bytes 12680 | tf_op jit(solution)/shard_map/ppermute | solution.py:27
  20.8 6.9 %collective-permute-start.13 = (f32[1,264,4]{2,1,0:T(8,128)S(1)}, f32[1,264,4]{2,1,0:T(8,128)S(1)}, u32[]{:S(2)}, u32[]{:S(2)}) collective-permute-start(f32[1,264,4]{2,1,0:T(8,128)S(1)} %get-tuple-element.40), channel_id=1, source_target_pairs={{1,0},{3,2},{5,4},{7,6},{9,8},{11,10},{13,12},{15,14},{17,16},{19,... | collective-permute-start | bytes 12680 | tf_op jit(solution)/shard_map/ppermute | solution.py:28
  22.1 6.8 %collective-permute-start.1 = (f32[1,1,256]{2,1,0:T(1,128)S(1)}, f32[1,1,256]{2,1,0:T(1,128)S(1)}, u32[]{:S(2)}, u32[]{:S(2)}) collective-permute-start(f32[1,1,256]{2,1,0:T(1,128)S(1)} %get-tuple-element.45), channel_id=1, source_target_pairs={{0,2},{2,4},{4,6},{1,3},{3,5},{5,7},{8,10},{10,12},{12,14},{9,11},... | collective-permute-start | bytes 3080 | tf_op jit(solution)/shard_map/ppermute | solution.py:27
  30.8 7.0 %collective-permute-start.3 = (f32[1,258,1]{2,1,0:T(8,128)S(1)}, f32[1,258,1]{2,1,0:T(8,128)S(1)}, u32[]{:S(2)}, u32[]{:S(2)}) collective-permute-start(f32[1,258,1]{2,1,0:T(8,128)S(1)} %get-tuple-element.41), channel_id=1, source_target_pairs={{1,0},{3,2},{5,4},{7,6},{9,8},{11,10},{13,12},{15,14},{17,16},{19,... | collective-permute-start | bytes 3104 | tf_op jit(solution)/shard_map/ppermute | solution.py:28
  32.1 6.6 %collective-permute-start.4 = (f32[1,258,1]{2,1,0:T(8,128)S(1)}, f32[1,258,1]{2,1,0:T(8,128)S(1)}, u32[]{:S(2)}, u32[]{:S(2)}) collective-permute-start(f32[1,258,1]{2,1,0:T(8,128)S(1)} %get-tuple-element.42), channel_id=1, source_target_pairs={{0,1},{2,3},{4,5},{6,7},{8,9},{10,11},{12,13},{14,15},{16,17},{18,... | collective-permute-start | bytes 3104 | tf_op jit(solution)/shard_map/ppermute | solution.py:27
  39.7 5.7 %collective-permute-start.5 = (f32[5,1,4,256]{3,2,1,0:T(4,128)S(1)}, f32[5,1,4,256]{3,2,1,0:T(4,128)S(1)}, u32[]{:S(2)}, u32[]{:S(2)}) collective-permute-start(f32[5,1,4,256]{3,2,1,0:T(4,128)S(1)} %get-tuple-element.27), channel_id=1, source_target_pairs={{0,2},{2,4},{4,6},{1,3},{3,5},{5,7},{8,10},{10,12},{12,14},{9,11},... | collective-permute-start | bytes 61448 | tf_op jit(solution)/shard_map/ppermute | solution.py:27
  42.9 4.5 %collective-permute-start.6 = (f32[5,1,4,256]{3,2,1,0:T(4,128)S(1)}, f32[5,1,4,256]{3,2,1,0:T(4,128)S(1)}, u32[]{:S(2)}, u32[]{:S(2)}) collective-permute-start(f32[5,1,4,256]{3,2,1,0:T(4,128)S(1)} %get-tuple-element.28), channel_id=1, source_target_pairs={{2,0},{4,2},{6,4},{3,1},{5,3},{7,5},{10,8},{12,10},{14,12},{11,9},... | collective-permute-start | bytes 61448 | tf_op jit(solution)/shard_map/ppermute | solution.py:28
  50.2 8.0 %collective-permute-start.7 = (f32[5,1,264,4]{2,3,1,0:T(4,128)S(1)}, f32[5,1,264,4]{2,3,1,0:T(4,128)S(1)}, u32[]{:S(2)}, u32[]{:S(2)}) collective-permute-start(f32[5,1,264,4]{2,3,1,0:T(4,128)S(1)} %copy.15), channel_id=1, source_target_pairs={{0,1},{2,3},{4,5},{6,7},{8,9},{10,11},{12,13},{14,15},{16,17},{18,... | collective-permute-start | bytes 63368 | tf_op jit(solution)/shard_map/ppermute | solution.py:27
  55.8 4.7 %collective-permute-start.8 = (f32[5,1,264,4]{2,3,1,0:T(4,128)S(1)}, f32[5,1,264,4]{2,3,1,0:T(4,128)S(1)}, u32[]{:S(2)}, u32[]{:S(2)}) collective-permute-start(f32[5,1,264,4]{2,3,1,0:T(4,128)S(1)} %copy.16), channel_id=1, source_target_pairs={{1,0},{3,2},{5,4},{7,6},{9,8},{11,10},{13,12},{15,14},{17,16},{19,... | collective-permute-start | bytes 63368 | tf_op jit(solution)/shard_map/ppermute | solution.py:28
  68.9 22.5 %collective-permute-start.9 = (f32[5,1,256,256]{3,2,1,0:T(8,128)}, f32[5,1,256,256]{3,2,1,0:T(8,128)S(1)}, u32[]{:S(2)}, u32[]{:S(2)}) collective-permute-start(f32[5,1,256,256]{3,2,1,0:T(8,128)} %fusion), channel_id=1, source_target_pairs={{8,0},{16,8},{24,16},{9,1},{17,9},{25,17},{10,2},{18,10},{26,18},{... | collective-permute-start | bytes 3932168 | tf_op jit(solution)/shard_map/ppermute | solution.py:17
  81.8 4.7 %collective-permute-start.20 = (f32[4,1,264,4]{2,3,1,0:T(4,128)S(1)}, f32[4,1,264,4]{2,3,1,0:T(4,128)S(1)}, u32[]{:S(2)}, u32[]{:S(2)}) collective-permute-start(f32[4,1,264,4]{2,3,1,0:T(4,128)S(1)} %copy.27), channel_id=1, source_target_pairs={{0,1},{2,3},{4,5},{6,7},{8,9},{10,11},{12,13},{14,15},{16,17},{18,... | collective-permute-start | bytes 50696 | tf_op jit(solution)/shard_map/ppermute | solution.py:27
  84.2 5.0 %collective-permute-start.21 = (f32[4,1,264,4]{2,3,1,0:T(4,128)S(1)}, f32[4,1,264,4]{2,3,1,0:T(4,128)S(1)}, u32[]{:S(2)}, u32[]{:S(2)}) collective-permute-start(f32[4,1,264,4]{2,3,1,0:T(4,128)S(1)} %copy.28), channel_id=1, source_target_pairs={{1,0},{3,2},{5,4},{7,6},{9,8},{11,10},{13,12},{15,14},{17,16},{19,... | collective-permute-start | bytes 50696 | tf_op jit(solution)/shard_map/ppermute | solution.py:28
  91.5 6.9 %collective-permute-start.14 = (f32[5,1,3,256]{3,1,2,0:T(1,128)S(1)}, f32[5,1,3,256]{3,1,2,0:T(1,128)S(1)}, u32[]{:S(2)}, u32[]{:S(2)}) collective-permute-start(f32[5,1,3,256]{3,1,2,0:T(1,128)S(1)} %copy.19), channel_id=1, source_target_pairs={{0,2},{2,4},{4,6},{1,3},{3,5},{5,7},{8,10},{10,12},{12,14},{9,11},... | collective-permute-start | bytes 46088 | tf_op jit(solution)/shard_map/ppermute | solution.py:27
  102.2 8.3 %collective-permute-start.16 = (f32[5,1,262,3]{2,0,3,1:T(8,128)S(1)}, f32[5,1,262,3]{2,0,3,1:T(8,128)S(1)}, u32[]{:S(2)}, u32[]{:S(2)}) collective-permute-start(f32[5,1,262,3]{2,0,3,1:T(8,128)S(1)} %copy.23), channel_id=1, source_target_pairs={{0,1},{2,3},{4,5},{6,7},{8,9},{10,11},{12,13},{14,15},{16,17},{18,... | collective-permute-start | bytes 47168 | tf_op jit(solution)/shard_map/ppermute | solution.py:27
  106.2 5.4 %collective-permute-start.17 = (f32[5,1,262,3]{2,0,3,1:T(8,128)S(1)}, f32[5,1,262,3]{2,0,3,1:T(8,128)S(1)}, u32[]{:S(2)}, u32[]{:S(2)}) collective-permute-start(f32[5,1,262,3]{2,0,3,1:T(8,128)S(1)} %copy.24), channel_id=1, source_target_pairs={{1,0},{3,2},{5,4},{7,6},{9,8},{11,10},{13,12},{15,14},{17,16},{19,... | collective-permute-start | bytes 47168 | tf_op jit(solution)/shard_map/ppermute | solution.py:28
  126.4 10.8 %collective-permute-start.22 = (f32[2,1,256,256]{3,2,1,0:T(8,128)S(1)}, f32[2,1,256,256]{3,2,1,0:T(8,128)S(1)}, u32[]{:S(2)}, u32[]{:S(2)}) collective-permute-start(f32[2,1,256,256]{3,2,1,0:T(8,128)S(1)} %pad_maximum_fusion.14), channel_id=1, source_target_pairs={{0,8},{8,16},{16,24},{1,9},{9,17},{17,25},{2,10},{10,18},{18,26},{... | collective-permute-start | bytes 1572872 | tf_op jit(solution)/shard_map/ppermute | solution.py:17
  131.1 10.5 %collective-permute-start.23 = (f32[2,1,256,256]{3,2,1,0:T(8,128)S(1)}, f32[2,1,256,256]{3,2,1,0:T(8,128)S(1)}, u32[]{:S(2)}, u32[]{:S(2)}) collective-permute-start(f32[2,1,256,256]{3,2,1,0:T(8,128)S(1)} %pad_maximum_fusion.14), channel_id=1, source_target_pairs={{8,0},{16,8},{24,16},{9,1},{17,9},{25,17},{10,2},{18,10},{26,18},{... | collective-permute-start | bytes 1572872 | tf_op jit(solution)/shard_map/ppermute | solution.py:17
  151.4 7.8 %collective-permute-start.26 = (f32[4,1,264,4]{2,3,1,0:T(4,128)S(1)}, f32[4,1,264,4]{2,3,1,0:T(4,128)}, u32[]{:S(2)}, u32[]{:S(2)}) collective-permute-start(f32[4,1,264,4]{2,3,1,0:T(4,128)S(1)} %copy.31), channel_id=1, source_target_pairs={{0,1},{2,3},{4,5},{6,7},{8,9},{10,11},{12,13},{14,15},{16,17},{18,... | collective-permute-start | bytes 50696 | tf_op jit(solution)/shard_map/ppermute | solution.py:27
  157.7 5.1 %collective-permute-start.27 = (f32[4,1,264,4]{2,3,1,0:T(4,128)}, f32[4,1,264,4]{2,3,1,0:T(4,128)}, u32[]{:S(2)}, u32[]{:S(2)}) collective-permute-start(f32[4,1,264,4]{2,3,1,0:T(4,128)} %copy.32), channel_id=1, source_target_pairs={{1,0},{3,2},{5,4},{7,6},{9,8},{11,10},{13,12},{15,14},{17,16},{19,... | collective-permute-start | bytes 50696 | tf_op jit(solution)/shard_map/ppermute | solution.py:28
  (56 other events, 313.4 us)
where the time goes:
time: 179 us; the launch traced here: 177 us
  starting transfers between devices  74.4 us (42%)
  local copies, waits for them, and re-layouts  42.6 us (24%)
  other arithmetic  34.7 us (19%)
  waiting for transfers between devices  23.7 us (13%)
    ppermute x12, starting transfers between devices, extended(): before = lax.ppermute(last, axis, up)  41.4 us
    ppermute x4, starting transfers between devices, from_behind(): lax.ppermute(value, axis, [(source, source + steps) for source in range(f...  17 us
    ppermute x12, starting transfers between devices, extended(): after = lax.ppermute(first, axis, down)  15.9 us
    ppermute x12, waiting for transfers between devices, extended(): after = lax.ppermute(first, axis, down)  13.1 us
    slice x14, local copies, waits for them, and re-layouts, extended(): last = lax.slice_in_dim(x, length - width, length, axis=dim)  11.4 us
    concatenate x11, other arithmetic, extended(): x = jnp.concatenate([before, x, after], axis=dim)  11.3 us
    ppermute x4, waiting for transfers between devices, from_behind(): lax.ppermute(value, axis, [(source, source + steps) for source in range(f...  9.66 us
    another operation x14, other arithmetic, jacobi(): return jnp.stack([new_x, new_y])  8.91 us
  transfers between devices with their start and end apart: 28, of which 12 were waited for; matrix products, arithmetic and copies ran while one was open for 23% of the time, Pallas kernels for 0%

commit v1 on v0

v1 whole, which is shorter than its diff:
```python
import functools

import jax
import jax.numpy as jnp
from jax import lax
from jax.experimental import pallas as pl
from jax.experimental.pallas import tpu as pltpu
from jax.sharding import PartitionSpec as P

RADIUS = 4
SWEEPS = 4
ROUNDS = 2
COUPLING = 0.25
MESH = pl.DeviceIdType.MESH

LANES = 128
HALO = 16
EDGE = HALO + 8
SLOT = 16
FOLD = LANES // (2 * SLOT)

TILE_B = 0
ROW_A_UP, ROW_A_DOWN, ROW_S_UP, ROW_S_DOWN = 1, 2, 3, 4
COL_RIGHT, COL_LEFT = 5, 6
FWD_TOP, FWD_BOTTOM, FWD_RIGHT, FWD_LEFT = 7, 8, 9, 10
FIELD_NEXT, FIELD_PREV, RIM_NEXT, RIM_PREV = 11, 12, 13, 14
COPIES = 15


def lane_roll(x, shift):
    return pltpu.roll(x, shift % x.shape[1], 1)


def window_sum(x, axis):
    size = x.shape[axis]
    two = x + pltpu.roll(x, 1, axis)
    four = two + pltpu.roll(two, 2, axis)
    return x + (pltpu.roll(four, 1, axis) + pltpu.roll(four, size - 4, axis))


def stacked(block):
    rows = block.shape[0]
    return tuple(
        x[8 : rows - 8, :] for x in (pltpu.roll(block, 1, 0), block, pltpu.roll(block, rows - 1, 0))
    )


def kernel(
    counts, images, stiff, tensor_out, field_out,
    a, b, s, ku, kd, kl, kr, ks, gx, gy, pr, tt, ca, cb, cc, bx, by, f0, f1,
    send_right, send_left, got_left, got_right, next_left, next_right,
    rim, rim_before, rim_after, main_before, main_after,
    local_sem, send_sem, recv_sem,
):
    sec, row, col = (lax.axis_index(name) for name in ("sec", "row", "col"))
    n_sec, n_row, n_col = counts
    rows, width = images.shape[1], images.shape[2]
    total, wide = a.shape
    has_prev, has_next = sec > 0, sec < n_sec - 1
    has_up, has_down = row > 0, row < n_row - 1
    has_left, has_right = col > 0, col < n_col - 1
    sides = (
        (has_prev, (sec - 1, row, col)), (has_next, (sec + 1, row, col)),
        (has_up, (sec, row - 1, col)), (has_down, (sec, row + 1, col)),
        (has_left, (sec, row, col - 1)), (has_right, (sec, row, col + 1)),
    )
    prev_id, next_id, up_id, down_id, left_id, right_id = (side[1] for side in sides)
    end = EDGE + rows
    first, last = 8, total - 8
    inner = pl.ds(EDGE, rows)
    main = pl.ds(0, width)
    top, bottom = pl.ds(EDGE - HALO, HALO), pl.ds(end, HALO)
    piece = (last - first) // FOLD

    def remote(src, dst, k, device):
        return pltpu.make_async_remote_copy(
            src_ref=src, dst_ref=dst, send_sem=send_sem.at[k], recv_sem=recv_sem.at[k],
            device_id=device, device_id_type=MESH,
        )

    load_a = pltpu.make_async_copy(images.at[0], a.at[inner, main], local_sem.at[0])
    load_s = pltpu.make_async_copy(stiff.at[0], s.at[inner, main], local_sem.at[1])
    load_a.start()
    load_s.start()
    barrier = pltpu.get_barrier_semaphore()
    for there, device in sides:
        @pl.when(there)
        def _():
            pl.semaphore_signal(barrier, inc=1, device_id=device, device_id_type=MESH)

    def clear(ref):
        ref[...] = jnp.zeros(ref.shape, jnp.float32)

    @pl.when(jnp.logical_not(has_up))
    def _():
        clear(a.at[top, main])
        clear(s.at[top, main])

    @pl.when(jnp.logical_not(has_down))
    def _():
        clear(a.at[bottom, main])
        clear(s.at[bottom, main])

    @pl.when(jnp.logical_not(has_left))
    def _():
        clear(got_left)

    @pl.when(jnp.logical_not(has_right))
    def _():
        clear(got_right)

    @pl.when(jnp.logical_not(has_next))
    def _():
        clear(b)
        clear(next_left)
        clear(next_right)
        clear(rim_after)
        clear(main_after)

    @pl.when(jnp.logical_not(has_prev))
    def _():
        clear(rim_before)
        clear(main_before)

    for ref in (a, s):
        clear(ref.at[pl.ds(0, 8), :])
        clear(ref.at[pl.ds(total - 8, 8), :])
    for ref in (f0, f1):
        for part in range(2):
            clear(ref.at[part, pl.ds(8, 8), :])
            clear(ref.at[part, pl.ds(total - 16, 8), :])

    pl.semaphore_wait(barrier, sum(jnp.where(there, 1, 0) for there, _device in sides))

    tile_b = remote(images.at[0], b.at[inner, main], TILE_B, prev_id)
    a_up = remote(images.at[0, pl.ds(0, HALO)], a.at[bottom, main], ROW_A_UP, up_id)
    s_up = remote(stiff.at[0, pl.ds(0, HALO)], s.at[bottom, main], ROW_S_UP, up_id)
    a_down = remote(images.at[0, pl.ds(rows - HALO, HALO)], a.at[top, main], ROW_A_DOWN, down_id)
    s_down = remote(stiff.at[0, pl.ds(rows - HALO, HALO)], s.at[top, main], ROW_S_DOWN, down_id)
    fwd_top = remote(a.at[top, main], b.at[top, main], FWD_TOP, prev_id)
    fwd_bottom = remote(a.at[bottom, main], b.at[bottom, main], FWD_BOTTOM, prev_id)
    col_right = remote(send_right, got_left, COL_RIGHT, right_id)
    col_left = remote(send_left, got_right, COL_LEFT, left_id)
    fwd_left = remote(got_left, next_left, FWD_LEFT, prev_id)
    fwd_right = remote(got_right, next_right, FWD_RIGHT, prev_id)

    @pl.when(has_up)
    def _():
        a_up.start()
        s_up.start()

    @pl.when(has_down)
    def _():
        a_down.start()
        s_down.start()

    @pl.when(has_prev)
    def _():
        tile_b.start()

    load_a.wait()
    load_s.wait()

    @pl.when(has_up)
    def _():
        a_down.wait_recv()
        s_down.wait_recv()

    @pl.when(has_down)
    def _():
        a_up.wait_recv()
        s_up.wait_recv()

    @pl.when(has_prev)
    def _():
        fwd_top.start()
        fwd_bottom.start()

    def lanes_of(shape):
        return lax.broadcasted_iota(jnp.int32, shape, 1)

    lane = lanes_of((piece, LANES))

    def packed(ref_low, ref_high, column, at):
        out = jnp.zeros((piece, LANES), jnp.float32)
        for j in range(FOLD):
            span = pl.ds(first + j * piece, piece)
            for k, ref in enumerate((ref_low, ref_high)):
                low = (2 * j + k) * SLOT
                moved = lane_roll(ref[span, column], low - at)
                out = jnp.where((lane >= low) & (lane < low + SLOT), moved, out)
        return out

    def unpack(ref, left, right, k):
        for j in range(FOLD):
            low = (2 * j + k) * SLOT
            span = pl.ds(first + j * piece, piece)
            from_right = jnp.where(lane < SLOT, lane_roll(right[...], -low), 0.0)
            from_left = lane_roll(left[...], LANES - SLOT - low)
            ref[span, pl.ds(width, LANES)] = jnp.where(lane >= LANES - SLOT, from_left, from_right)

    @pl.when(has_right)
    def _():
        send_right[...] = packed(a, s, pl.ds(width - LANES, LANES), LANES - SLOT)
        col_right.start()

    @pl.when(has_left)
    def _():
        send_left[...] = packed(a, s, pl.ds(0, LANES), 0)
        col_left.start()

    @pl.when(has_left)
    def _():
        col_right.wait_recv()

    @pl.when(has_right)
    def _():
        col_left.wait_recv()

    @pl.when(has_prev)
    def _():
        fwd_left.start()
        fwd_right.start()

    unpack(a, got_left, got_right, 0)
    unpack(s, got_left, got_right, 1)

    step = 16

    def blocks(low, high, body):
        def one(i, carry):
            body(pl.multiple_of(low + i * step, 8))
            return carry

        lax.fori_loop(0, (high - low) // step, one, 0)

    lane_wide = lanes_of((step, wide))
    middle = width + LANES // 2
    lane_ok = (
        (lane_wide < width)
        | ((lane_wide < middle) & has_right)
        | ((lane_wide >= middle) & has_left)
    )
    row_in = lax.broadcasted_iota(jnp.int32, (step, wide), 0)

    def gradient_block(r):
        at = pl.ds(r, step)
        rr = row_in + r
        ok = lane_ok & ((rr >= EDGE) | has_up) & ((rr < end) | has_down)
        up, mid, down = stacked(a[pl.ds(r - 8, step + 16), :])
        dx = jnp.where(ok, (lane_roll(mid, -1) - lane_roll(mid, 1)) * 0.5, 0.0)
        dy = jnp.where(ok, (down - up) * 0.5, 0.0)
        gx[at, :] = dx
        gy[at, :] = dy
        pr[0, at, :] = dx * dx
        pr[1, at, :] = dx * dy
        pr[2, at, :] = dy * dy

    blocks(first, last, gradient_block)

    def kappa_block(r):
        at = pl.ds(r, step)
        above, mid, below = stacked(s[pl.ds(r - 8, step + 16), :])
        up = jnp.sqrt(mid * above)
        down = jnp.sqrt(mid * below)
        left = jnp.sqrt(mid * lane_roll(mid, 1))
        right = lane_roll(left, -1)
        ku[at, :] = up
        kd[at, :] = down
        kl[at, :] = left
        kr[at, :] = right
        ks[at, :] = up + down + left + right + 2.0 * COUPLING

    blocks(16, total - 16, kappa_block)

    @pl.when(has_next)
    def _():
        tile_b.wait_recv()
        fwd_top.wait_recv()
        fwd_bottom.wait_recv()
        fwd_left.wait_recv()
        fwd_right.wait_recv()

    unpack(b, next_left, next_right, 0)

    def change_block(r):
        at = pl.ds(r, step)
        change = b[at, :] - a[at, :]
        pr[3, at, :] = gx[at, :] * change
        pr[4, at, :] = gy[at, :] * change

    blocks(first, last, change_block)

    scale = jnp.where(has_next, jnp.float32(1.0), jnp.float32(0.0))
    cells = float((2 * RADIUS + 1) ** 2)

    def tensor_block(r):
        at = pl.ds(r, step)
        parts = []
        for k in range(5):
            around = pr[k, pl.ds(r - 8, step + 16), :]
            summed = window_sum(around, 0)[8 : 8 + step, :]
            value = window_sum(summed, 1) * (scale / cells)
            tt[k, at, :] = value
            parts.append(value)
        xx, xy, yy, xt, yt = parts
        diag = ks[at, :]
        one, two = xx + diag, yy + diag
        inverse = 1.0 / (one * two - xy * xy)
        va, vb, vc = two * inverse, xy * inverse, one * inverse
        ca[at, :] = va
        cb[at, :] = vb
        cc[at, :] = vc
        f0[0, at, :] = vb * yt - va * xt
        f0[1, at, :] = vb * xt - vc * yt

    blocks(16, total - 16, tensor_block)
    put_tensor = pltpu.make_async_copy(
        tt.at[:, inner, main], tensor_out.at[:, 0], local_sem.at[0]
    )
    put_tensor.start()

    def sweep(source, target, right_x, right_y):
        def body(r):
            at = pl.ds(r, step)
            vu, vd, vl, vr = ku[at, :], kd[at, :], kl[at, :], kr[at, :]

            def near(part):
                up, mid, down = stacked(source[part, pl.ds(r - 8, step + 16), :])
                return (
                    vu * up + vd * down
                    + vl * lane_roll(mid, 1) + vr * lane_roll(mid, -1)
                )

            rx = near(0) + right_x(at)
            ry = near(1) + right_y(at)
            va, vb, vc = ca[at, :], cb[at, :], cc[at, :]
            target[0, at, :] = va * rx - vb * ry
            target[1, at, :] = vc * ry - vb * rx

        blocks(16, total - 16, body)

    for k in range(SWEEPS - 1):
        source, target = (f0, f1) if k % 2 == 0 else (f1, f0)
        sweep(source, target, lambda at: -tt[3, at, :], lambda at: -tt[4, at, :])
    now, other = (f1, f0) if (SWEEPS - 1) % 2 == 1 else (f0, f1)

    span = pl.ds(16, total - 32)
    rim[...] = packed_rim(now, piece, first, width, lane)
    field_next = remote(now.at[:, span, main], main_before, FIELD_NEXT, next_id)
    field_prev = remote(now.at[:, span, main], main_after, FIELD_PREV, prev_id)
    rim_next = remote(rim, rim_before, RIM_NEXT, next_id)
    rim_prev = remote(rim, rim_after, RIM_PREV, prev_id)

    @pl.when(has_next)
    def _():
        rim_next.start()
        field_next.start()

    @pl.when(has_prev)
    def _():
        rim_prev.start()
        field_prev.start()

    @pl.when(has_prev)
    def _():
        rim_next.wait_recv()
        field_next.wait_recv()

    @pl.when(has_next)
    def _():
        rim_prev.wait_recv()
        field_prev.wait_recv()

    both = rim_before[...] + rim_after[...]
    for j in range(FOLD):
        at = pl.ds(first + j * piece, piece)
        for k, ref in enumerate((bx, by)):
            low = (2 * j + k) * SLOT
            head = jnp.where(lane < 8, lane_roll(both, -low), 0.0)
            tail = lane_roll(both, LANES - 16 - low)
            ref[at, pl.ds(width, LANES)] = jnp.where(lane >= LANES - 8, tail, head)

    def beside_block(r):
        at = pl.ds(r, step)
        there = pl.ds(pl.multiple_of(r - 16, 8), step)
        for part, ref in enumerate((bx, by)):
            ref[at, main] = (
                COUPLING * (main_before[part, there, :] + main_after[part, there, :])
                - tt[3 + part, at, main]
            )
            ref[at, pl.ds(width, LANES)] = (
                COUPLING * ref[at, pl.ds(width, LANES)] - tt[3 + part, at, pl.ds(width, LANES)]
            )

    blocks(16, total - 16, beside_block)

    @pl.when(has_next)
    def _():
        field_next.wait_send()
        rim_next.wait_send()

    @pl.when(has_prev)
    def _():
        field_prev.wait_send()
        rim_prev.wait_send()

    for k in range(SWEEPS):
        sweep(now, other, lambda at: bx[at, :], lambda at: by[at, :])
        now, other = other, now

    put_field = pltpu.make_async_copy(
        now.at[:, inner, main], field_out.at[:, 0], local_sem.at[1]
    )
    put_field.start()

    @pl.when(has_up)
    def _():
        a_up.wait_send()
        s_up.wait_send()

    @pl.when(has_down)
    def _():
        a_down.wait_send()
        s_down.wait_send()

    @pl.when(has_right)
    def _():
        col_right.wait_send()

    @pl.when(has_left)
    def _():
        col_left.wait_send()

    @pl.when(has_prev)
    def _():
        for copy in (tile_b, fwd_top, fwd_bottom, fwd_left, fwd_right):
            copy.wait_send()

    put_tensor.wait()
    put_field.wait()


def packed_rim(field, piece, first, width, lane):
    out = jnp.zeros((piece, LANES), jnp.float32)
    for j in range(FOLD):
        at = pl.ds(first + j * piece, piece)
        for k in range(2):
            low = (2 * j + k) * SLOT
            block = field[k, at, pl.ds(width, LANES)]
            head = lane_roll(block, low)
            tail = lane_roll(block, low + SLOT)
            out = jnp.where((lane >= low) & (lane < low + 8), head, out)
            out = jnp.where((lane >= low + 8) & (lane < low + 16), tail, out)
    return out


def local(counts, images, stiffness):
    _, rows, width = images.shape
    total, wide = rows + 2 * EDGE, width + LANES
    piece = (total - 16) // FOLD
    f32 = jnp.float32
    plane = pltpu.VMEM((total, wide), f32)
    packet = pltpu.VMEM((piece, LANES), f32)
    pair = pltpu.VMEM((2, total, wide), f32)
    mains = pltpu.VMEM((2, total - 32, width), f32)
    return pl.pallas_call(
        functools.partial(kernel, counts),
        out_shape=(
            jax.ShapeDtypeStruct((5, 1, rows, width), f32),
            jax.ShapeDtypeStruct((2, 1, rows, width), f32),
        ),
        in_specs=[pl.BlockSpec(memory_space=pl.ANY)] * 2,
        out_specs=[pl.BlockSpec(memory_space=pl.ANY)] * 2,
        scratch_shapes=[plane] * 10
        + [pltpu.VMEM((5, total, wide), f32)] * 2
        + [plane] * 5
        + [pair] * 2
        + [packet] * 9
        + [mains] * 2
        + [
            pltpu.SemaphoreType.DMA((2,)),
            pltpu.SemaphoreType.DMA((COPIES,)),
            pltpu.SemaphoreType.DMA((COPIES,)),
        ],
        compiler_params=pltpu.CompilerParams(
            collective_id=0, has_side_effects=True, vmem_limit_bytes=48 * 1024 * 1024
        ),
    )(images, stiffness)


def solution(mesh):
    counts = tuple(mesh.shape[name] for name in ("sec", "row", "col"))
    spec = P("sec", "row", "col")
    out = P(None, "sec", "row", "col")
    return jax.shard_map(
        functools.partial(local, counts), mesh=mesh, in_specs=(spec, spec),
        out_specs=(out, out), check_vma=False,
    )
```

time: 179 us -> 47 us (0.26); the launches traced: 177 us -> 46.8 us
  starting transfers between devices: 74.4 us -> 0 us
  Pallas kernels: 0 us -> 42.4 us
  local copies, waits for them, and re-layouts: 42.6 us -> 3.74 us
  other arithmetic: 34.7 us -> 0 us
  waiting for transfers between devices: 23.7 us -> 0 us
    ppermute x28 -> x0, starting transfers between devices: 74.4 us -> none  [the longest x12 41.4 us: extended(): before = lax.ppermute(last, axis, up)]
    pallas_call x0 -> x1, Pallas kernels: none -> 42.4 us  [local(): pl.pallas_call(functools.partial(kernel, counts), out_shape=(jax.ShapeDty...]
    ppermute x28 -> x0, waiting for transfers between devices: 23.7 us -> none  [the longest x12 13.1 us: extended(): after = lax.ppermute(first, axis, down)]
    slice x20 -> x0, local copies, waits for them, and re-layouts: 16.6 us -> none  [the longest x14 11.4 us: extended(): last = lax.slice_in_dim(x, length - width, length, axis=dim)]
    concatenate x11 -> x0, other arithmetic: 11.3 us -> none  [extended(): x = jnp.concatenate([before, x, after], axis=dim)]
    ppermute x10 -> x0, local copies, waits for them, and re-layouts: 10.4 us -> none  [the longest x5 5.25 us: extended(): before = lax.ppermute(last, axis, up)]
    add x10 -> x0, other arithmetic: 9.24 us -> none  [the longest x8 7.78 us: jacobi(): neighbour + kappas[2] * field_pad[..., 1:-1, :-2]]
    another operation x15 -> x0, other arithmetic: 9.01 us -> none  [the longest x14 8.91 us: jacobi(): return jnp.stack([new_x, new_y])]
  transfers between devices with their start and end apart: 28 -> 0, of which waited for: 12 -> 0; matrix products, arithmetic and copies ran while one was open for 23% -> 0% of each run, Pallas kernels for 0% -> 0%
where the time goes in v1:
time: 47 us; the launch traced here: 46.8 us
  Pallas kernels  42.4 us (90%)
  local copies, waits for them, and re-layouts  3.74 us (8%)
  between operations  0.65 us (1%)
    pallas_call x1, Pallas kernels, local(): pl.pallas_call(functools.partial(kernel, counts), out_shape=(jax.ShapeDty...  42.4 us
    unnamed x6, local copies, waits for them, and re-layouts  3.74 us

profile of v1, /device:TPU:1, one launch (start us, length us, event | category | flops | bytes accessed | tf_op | source)
XLA Modules:
  0.0 46.8 jit_solution(10449318208487706821)
XLA Ops:
  0.6 0.0 copy-start
  0.6 0.9 %copy-done = f32[1,256,256]{2,1,0:T(8,128)S(1)} copy-done((f32[1,256,256]{2,1,0:T(8,128)S(1)}, f32[1,256,256]{2,1,0:T(8,128)}, u32[]{:S(2)}) %copy-start) | copy-done | bytes 262168
  1.6 0.0 copy-start.1
  1.6 0.9 %copy-done.1 = f32[1,256,256]{2,1,0:T(8,128)S(1)} copy-done((f32[1,256,256]{2,1,0:T(8,128)S(1)}, f32[1,256,256]{2,1,0:T(8,128)}, u32[]{:S(2)}) %copy-start.1) | copy-done | bytes 262168
  2.5 42.4 %shard_map.41 = (f32[5,1,256,256]{3,2,1,0:T(8,128)S(1)}, f32[2,1,256,256]{3,2,1,0:T(8,128)S(1)}) custom-call(f32[1,256,256]{2,1,0:T(8,128)S(1)} %copy-done, f32[1,256,256]{2,1,0:T(8,128)S(1)} %copy-done.1), custom_call_target="tpu_custom_call" | custom-call | tf_op jit(solution)/shard_map/pallas_call | solution.py:467
  45.0 1.1 %copy.6 = f32[5,1,256,256]{3,2,1,0:T(8,128)} copy(f32[5,1,256,256]{3,2,1,0:T(8,128)S(1)} %get-tuple-element.4) | data formatting | bytes 2621440
  46.0 0.8 %copy.7 = f32[2,1,256,256]{3,2,1,0:T(8,128)} copy(f32[2,1,256,256]{3,2,1,0:T(8,128)S(1)} %get-tuple-element.5) | data formatting | bytes 1048576
Async XLA Ops:
  0.6 1.0 %copy-start = (f32[1,256,256]{2,1,0:T(8,128)S(1)}, f32[1,256,256]{2,1,0:T(8,128)}, u32[]{:S(2)}) copy-start(f32[1,256,256]{2,1,0:T(8,128)} %images.1) | copy-start | bytes 786436
  1.6 0.9 %copy-start.1 = (f32[1,256,256]{2,1,0:T(8,128)S(1)}, f32[1,256,256]{2,1,0:T(8,128)}, u32[]{:S(2)}) copy-start(f32[1,256,256]{2,1,0:T(8,128)} %stiff.1) | copy-start | bytes 786436

commit v2 on v0

v2 whole, which is shorter than its diff:
```python
import functools

import jax
import jax.numpy as jnp
from jax import lax
from jax.experimental import pallas as pl
from jax.experimental.pallas import tpu as pltpu
from jax.sharding import PartitionSpec as P

RADIUS = 4
SWEEPS = 4
ROUNDS = 2
COUPLING = 0.25
MESH = pl.DeviceIdType.MESH

LANES = 128
HALO = 16
EDGE = HALO + 8
SLOT = 16
FOLD = LANES // (2 * SLOT)

(
    TILE_B, ROW_A_UP, ROW_A_DOWN, ROW_S_UP, ROW_S_DOWN, FWD_TOP, FWD_BOTTOM, COL_RIGHT, COL_LEFT,
    FWD_RIGHT, FWD_LEFT, FIELD_NEXT, FIELD_PREV, RIM_NEXT, RIM_PREV,
) = range(15)
KINDS = 15


def lane_roll(x, shift):
    return pltpu.roll(x, shift % x.shape[1], 1)


def shifted(blocks, shift, lane):
    rolled = [lane_roll(x, shift) for x in blocks]
    out = []
    for k, here in enumerate(rolled):
        if shift > 0:
            out.append(jnp.where(lane < shift, rolled[k - 1], here))
        else:
            out.append(jnp.where(lane >= LANES + shift, rolled[(k + 1) % len(rolled)], here))
    return out


def add(*terms):
    return [sum(xs[1:], xs[0]) for xs in zip(*terms)]


def kernel(
    counts, images, stiff, tensor_out, field_out,
    a, b, s, q, gx, gy, pr, p3, tt, ua, ub, uc, va, vb, vc, ex, ey, g0, g1, field,
    send_right, send_left, got_left, got_right, next_left, next_right,
    rim, rim_before, rim_after, main_before, main_after,
    local_sem, send_sem, recv_sem,
):
    sec, row, col = (lax.axis_index(name) for name in ("sec", "row", "col"))
    n_sec, n_row, n_col = counts
    rows, width = images.shape[1], images.shape[2]
    nb, total, _ = a.shape
    nw = nb - 1
    has_prev, has_next = sec > 0, sec < n_sec - 1
    has_up, has_down = row > 0, row < n_row - 1
    has_left, has_right = col > 0, col < n_col - 1
    sides = (
        (has_prev, (sec - 1, row, col)), (has_next, (sec + 1, row, col)),
        (has_up, (sec, row - 1, col)), (has_down, (sec, row + 1, col)),
        (has_left, (sec, row, col - 1)), (has_right, (sec, row, col + 1)),
    )
    prev_id, next_id, up_id, down_id, left_id, right_id = (side[1] for side in sides)
    end = EDGE + rows
    first, last = 8, total - 8
    inner = pl.ds(EDGE, rows)
    main = pl.ds(0, nw)
    top, bottom = pl.ds(EDGE - HALO, HALO), pl.ds(end, HALO)
    piece = (last - first) // FOLD

    def remote(src, dst, k, device, part=0):
        return pltpu.make_async_remote_copy(
            src_ref=src, dst_ref=dst, send_sem=send_sem.at[k, part],
            recv_sem=recv_sem.at[k, part], device_id=device, device_id_type=MESH,
        )

    def columns(k):
        return pl.ds(k * LANES, LANES)

    loads = [
        pltpu.make_async_copy(src.at[0, :, columns(k)], dst.at[k, inner], local_sem.at[i, k])
        for i, (src, dst) in enumerate(((images, a), (stiff, s)))
        for k in range(nw)
    ]
    for copy in loads:
        copy.start()
    barrier = pltpu.get_barrier_semaphore()
    for there, device in sides:
        @pl.when(there)
        def _():
            pl.semaphore_signal(barrier, inc=1, device_id=device, device_id_type=MESH)

    def clear(ref):
        ref[...] = jnp.zeros(ref.shape, jnp.float32)

    @pl.when(jnp.logical_not(has_up))
    def _():
        clear(a.at[main, top])
        clear(s.at[main, top])

    @pl.when(jnp.logical_not(has_down))
    def _():
        clear(a.at[main, bottom])
        clear(s.at[main, bottom])

    @pl.when(jnp.logical_not(has_left))
    def _():
        clear(got_left)

    @pl.when(jnp.logical_not(has_right))
    def _():
        clear(got_right)

    @pl.when(jnp.logical_not(has_next))
    def _():
        clear(b)
        clear(next_left)
        clear(next_right)
        clear(rim_after)
        clear(main_after)

    @pl.when(jnp.logical_not(has_prev))
    def _():
        clear(rim_before)
        clear(main_before)

    for start in (0, total - 8):
        clear(a.at[:, pl.ds(start, 8)])
    for start in (8, total - 16):
        for ref in (g0, g1, field):
            clear(ref.at[:, :, pl.ds(start, 8)])

    pl.semaphore_wait(barrier, sum(jnp.where(there, 1, 0) for there, _device in sides))

    def by_block(src, at, dst, to, k, device):
        return [
            remote(src.at[0, at, columns(p)], dst.at[p, to], k, device, p) for p in range(nw)
        ]

    low, high = pl.ds(0, HALO), pl.ds(rows - HALO, HALO)
    tile_b = by_block(images, pl.ds(0, rows), b, inner, TILE_B, prev_id)
    up = by_block(stiff, low, s, bottom, ROW_S_UP, up_id)
    up += by_block(images, low, a, bottom, ROW_A_UP, up_id)
    down = by_block(stiff, high, s, top, ROW_S_DOWN, down_id)
    down += by_block(images, high, a, top, ROW_A_DOWN, down_id)
    col_right = remote(send_right, got_left, COL_RIGHT, right_id)
    col_left = remote(send_left, got_right, COL_LEFT, left_id)
    forward_rows = [
        remote(a.at[main, top], b.at[main, top], FWD_TOP, prev_id),
        remote(a.at[main, bottom], b.at[main, bottom], FWD_BOTTOM, prev_id),
    ]
    forward_cols = [
        remote(got_left, next_left, FWD_LEFT, prev_id),
        remote(got_right, next_right, FWD_RIGHT, prev_id),
    ]

    def when_start(there, copies):
        @pl.when(there)
        def _():
            for copy in copies:
                copy.start()

    def when_got(there, copies):
        @pl.when(there)
        def _():
            for copy in copies:
                copy.wait_recv()

    def when_sent(there, copies):
        @pl.when(there)
        def _():
            for copy in copies:
                copy.wait_send()

    when_start(has_up, up)
    when_start(has_down, down)
    when_start(has_prev, tile_b)
    for copy in loads:
        copy.wait()
    when_got(has_up, down)
    when_got(has_down, up)
    when_start(has_prev, forward_rows)

    def lanes_of(count):
        return lax.broadcasted_iota(jnp.int32, (count, LANES), 1)

    lane = lanes_of(piece)

    def packed(block, at):
        out = jnp.zeros((piece, LANES), jnp.float32)
        for j in range(FOLD):
            span = pl.ds(first + j * piece, piece)
            for k, ref in enumerate((a, s)):
                low = (2 * j + k) * SLOT
                moved = lane_roll(ref[block, span, :], low - at)
                out = jnp.where((lane >= low) & (lane < low + SLOT), moved, out)
        return out

    def unpack(ref, left, right, k):
        for j in range(FOLD):
            low = (2 * j + k) * SLOT
            from_right = jnp.where(lane < SLOT, lane_roll(right[...], -low), 0.0)
            from_left = lane_roll(left[...], LANES - SLOT - low)
            ref[nw, pl.ds(first + j * piece, piece), :] = jnp.where(
                lane >= LANES - SLOT, from_left, from_right
            )

    @pl.when(has_right)
    def _():
        send_right[...] = packed(nw - 1, LANES - SLOT)
        col_right.start()

    @pl.when(has_left)
    def _():
        send_left[...] = packed(0, 0)
        col_left.start()

    when_got(has_left, [col_right])
    when_got(has_right, [col_left])
    when_start(has_prev, forward_cols)
    unpack(a, got_left, got_right, 0)
    unpack(s, got_left, got_right, 1)

    def blocks(low, high, step, body):
        def one(i, carry):
            body(pl.multiple_of(low + i * step, 8), step)
            return carry

        count = (high - low) // step
        lax.fori_loop(0, count, one, 0)
        rest = high - low - count * step
        if rest:
            body(low + count * step, rest)

    def get(ref, r, step, *lead):
        return [ref[(*lead, k, pl.ds(r, step), slice(None))] for k in range(nb)]

    def put(ref, values, r, step, *lead):
        for k, value in enumerate(values):
            ref[(*lead, k, pl.ds(r, step), slice(None))] = value

    def gradient_block(r, step):
        lane = lanes_of(step)
        rr = lax.broadcasted_iota(jnp.int32, (step, LANES), 0) + r
        row_ok = ((rr >= EDGE) | has_up) & ((rr < end) | has_down)
        rim_ok = ((lane < LANES // 2) & has_right) | ((lane >= LANES // 2) & has_left)
        masks = [row_ok] * nw + [row_ok & rim_ok]
        mid = get(a, r, step)
        after, before = shifted(mid, -1, lane), shifted(mid, 1, lane)
        under, over = get(a, r + 1, step), get(a, r - 1, step)
        dx = [jnp.where(m, (x - y) * 0.5, 0.0) for m, x, y in zip(masks, after, before)]
        dy = [jnp.where(m, (x - y) * 0.5, 0.0) for m, x, y in zip(masks, under, over)]
        put(gx, dx, r, step)
        put(gy, dy, r, step)
        put(pr, [x * x for x in dx], r, step, 0)
        put(pr, [x * y for x, y in zip(dx, dy)], r, step, 1)
        put(pr, [y * y for y in dy], r, step, 2)
        put(q, [jnp.sqrt(x) for x in get(s, r, step)], r, step)

    blocks(first, last, 16, gradient_block)

    def three_rows(k):
        def body(r, step):
            put(p3, add(*(get(pr, r + d, step, k) for d in (-1, 0, 1))), r, step, k)

        return body

    def three_first(r, step):
        for k in range(3):
            three_rows(k)(r, step)

    blocks(first, last, 16, three_first)

    when_got(has_next, tile_b + forward_rows + forward_cols)
    unpack(b, next_left, next_right, 0)

    def change_block(r, step):
        change = [x - y for x, y in zip(get(b, r, step), get(a, r, step))]
        put(pr, [x * y for x, y in zip(get(gx, r, step), change)], r, step, 3)
        put(pr, [x * y for x, y in zip(get(gy, r, step), change)], r, step, 4)

    blocks(first, last, 32, change_block)

    def three_second(r, step):
        for k in (3, 4):
            three_rows(k)(r, step)

    blocks(first, last, 16, three_second)

    scale = jnp.where(has_next, jnp.float32(1.0), jnp.float32(0.0))
    scale = scale * (1.0 / float((2 * RADIUS + 1) ** 2))

    def tensor_block(r, step):
        lane = lanes_of(step)
        parts = []
        for k in range(5):
            summed = add(*(get(p3, r + d, step, k) for d in (-3, 0, 3)))
            summed = add(summed, shifted(summed, 1, lane), shifted(summed, -1, lane))
            summed = add(summed, shifted(summed, 3, lane), shifted(summed, -3, lane))
            parts.append([x * scale for x in summed])
            put(tt, parts[-1], r, step, k)
        mid = get(q, r, step)
        around = add(
            get(q, r - 1, step), get(q, r + 1, step), shifted(mid, 1, lane), shifted(mid, -1, lane)
        )
        for k in range(nb):
            xx, xy, yy, xt, yt = (part[k] for part in parts)
            diag = mid[k] * around[k] + 2.0 * COUPLING
            one, two = xx + diag, yy + diag
            inverse = 1.0 / (one * two - xy * xy)
            ca, cb, cc = two * inverse, xy * inverse, one * inverse
            x, y = cb * yt - ca * xt, cb * xt - cc * yt
            at = pl.ds(r, step)
            for ref, value in ((va, ca), (vb, cb), (vc, cc)):
                ref[k, at, :] = value * COUPLING
            for ref, value in ((ua, ca), (ub, cb), (uc, cc)):
                ref[k, at, :] = value * mid[k]
            ex[k, at, :] = x
            ey[k, at, :] = y
            g0[0, k, at, :] = x * mid[k]
            g0[1, k, at, :] = y * mid[k]

    blocks(16, total - 16, 16, tensor_block)
    put_tensor = [
        pltpu.make_async_copy(
            tt.at[:, k, inner], tensor_out.at[:, 0, :, columns(k)], local_sem.at[0, k]
        )
        for k in range(nw)
    ]
    for copy in put_tensor:
        copy.start()

    def relaxed(source, r, step, x, y):
        lane = lanes_of(step)

        def near(part):
            mid = get(source, r, step, part)
            return add(
                get(source, r - 1, step, part), get(source, r + 1, step, part),
                shifted(mid, 1, lane), shifted(mid, -1, lane),
            )

        nx, ny = near(0), near(1)
        ca, cb, cc = (get(ref, r, step) for ref in (ua, ub, uc))
        return (
            [x[k] + ca[k] * nx[k] - cb[k] * ny[k] for k in range(nb)],
            [y[k] + cc[k] * ny[k] - cb[k] * nx[k] for k in range(nb)],
        )

    def sweep(source, target, final, low, high):
        def body(r, step):
            new = relaxed(source, r, step, get(ex, r, step), get(ey, r, step))
            if not final:
                mid = get(q, r, step)
                new = [[m * x for m, x in zip(mid, part)] for part in new]
            for part in range(2):
                put(target, new[part], r, step, part)

        blocks(low, high, 32, body)

    now, other = g0, g1
    for k in range(1, SWEEPS):
        final = k == SWEEPS - 1
        sweep(now, field if final else other, final, 16, total - 16)
        if not final:
            now, other = other, now

    span = pl.ds(16, total - 32)
    rim[...] = packed_rim(field, piece, first, nw, lane)
    to_next = [
        remote(rim, rim_before, RIM_NEXT, next_id),
        remote(field.at[:, main, span], main_before, FIELD_NEXT, next_id),
    ]
    to_prev = [
        remote(rim, rim_after, RIM_PREV, prev_id),
        remote(field.at[:, main, span], main_after, FIELD_PREV, prev_id),
    ]
    when_start(has_next, to_next)
    when_start(has_prev, to_prev)
    def scale_block(r, step):
        mid = get(q, r, step)
        for part in range(2):
            put(g0, [m * x for m, x in zip(mid, get(field, r, step, part))], r, step, part)

    blocks(16, total - 16, 32, scale_block)
    when_got(has_prev, to_next)
    when_got(has_next, to_prev)

    both = rim_before[...] + rim_after[...]
    for j in range(FOLD):
        for k, ref in enumerate((gx, gy)):
            low = (2 * j + k) * SLOT
            head = jnp.where(lane < 8, lane_roll(both, -low), 0.0)
            tail = lane_roll(both, LANES - 16 - low)
            ref[nw, pl.ds(first + j * piece, piece), :] = jnp.where(lane >= LANES - 8, tail, head)

    def first_block(r, step):
        there = pl.ds(r - 16, step)
        at = pl.ds(r, step)

        def beside(part, ref):
            return [
                main_before[part, k, there, :] + main_after[part, k, there, :] for k in range(nw)
            ] + [ref[nw, at, :]]

        x, y = beside(0, gx), beside(1, gy)
        ca, cb, cc = (get(ref, r, step) for ref in (va, vb, vc))
        old_x, old_y = get(ex, r, step), get(ey, r, step)
        new_x = [old_x[k] + ca[k] * x[k] - cb[k] * y[k] for k in range(nb)]
        new_y = [old_y[k] + cc[k] * y[k] - cb[k] * x[k] for k in range(nb)]
        put(ex, new_x, r, step)
        put(ey, new_y, r, step)
        mid = get(q, r, step)
        for part, values in enumerate(relaxed(g0, r, step, new_x, new_y)):
            put(g1, [m * v for m, v in zip(mid, values)], r, step, part)

    blocks(16, total - 16, 16, first_block)
    when_sent(has_next, to_next)
    when_sent(has_prev, to_prev)
    now, other = g1, g0
    for k in range(1, SWEEPS):
        final = k == SWEEPS - 1
        if final:
            sweep(now, field, final, EDGE, end)
        else:
            sweep(now, other, final, 16, total - 16)
        now, other = other, now

    put_field = [
        pltpu.make_async_copy(
            field.at[:, k, inner], field_out.at[:, 0, :, columns(k)], local_sem.at[1, k]
        )
        for k in range(nw)
    ]
    for copy in put_field:
        copy.start()
    when_sent(has_up, up)
    when_sent(has_down, down)
    when_sent(has_right, [col_right])
    when_sent(has_left, [col_left])
    when_sent(has_prev, tile_b + forward_rows + forward_cols)
    for copy in put_tensor + put_field:
        copy.wait()


def packed_rim(field, piece, first, nw, lane):
    out = jnp.zeros((piece, LANES), jnp.float32)
    for j in range(FOLD):
        at = pl.ds(first + j * piece, piece)
        for k in range(2):
            low = (2 * j + k) * SLOT
            block = field[k, nw, at, :]
            head = lane_roll(block, low)
            tail = lane_roll(block, low + SLOT)
            out = jnp.where((lane >= low) & (lane < low + 8), head, out)
            out = jnp.where((lane >= low + 8) & (lane < low + 16), tail, out)
    return out


def local(counts, images, stiffness):
    _, rows, width = images.shape
    nw = width // LANES
    nb = nw + 1
    total = rows + 2 * EDGE
    f32 = jnp.float32
    plane = pltpu.VMEM((nb, total, LANES), f32)
    five = pltpu.VMEM((5, nb, total, LANES), f32)
    pair = pltpu.VMEM((2, nb, total, LANES), f32)
    packet = pltpu.VMEM(((total - 16) // FOLD, LANES), f32)
    mains = pltpu.VMEM((2, nw, total - 32, LANES), f32)
    return pl.pallas_call(
        functools.partial(kernel, counts),
        out_shape=(
            jax.ShapeDtypeStruct((5, 1, rows, width), f32),
            jax.ShapeDtypeStruct((2, 1, rows, width), f32),
        ),
        in_specs=[pl.BlockSpec(memory_space=pltpu.HBM)] * 2,
        out_specs=[pl.BlockSpec(memory_space=pl.ANY)] * 2,
        scratch_shapes=[plane] * 6
        + [five] * 3
        + [plane] * 8
        + [pair] * 3
        + [packet] * 9
        + [mains] * 2
        + [
            pltpu.SemaphoreType.DMA((2, nw)),
            pltpu.SemaphoreType.DMA((KINDS, nw)),
            pltpu.SemaphoreType.DMA((KINDS, nw)),
        ],
        compiler_params=pltpu.CompilerParams(
            collective_id=0, has_side_effects=True, vmem_limit_bytes=48 * 1024 * 1024
        ),
    )(images, stiffness)


def solution(mesh):
    counts = tuple(mesh.shape[name] for name in ("sec", "row", "col"))
    spec = P("sec", "row", "col")
    out = P(None, "sec", "row", "col")
    return jax.shard_map(
        functools.partial(local, counts), mesh=mesh, in_specs=(spec, spec),
        out_specs=(out, out), check_vma=False,
    )
```

time: 179 us -> 40.2 us (0.22); the launches traced: 177 us -> 40.1 us
  starting transfers between devices: 74.4 us -> 0 us
  local copies, waits for them, and re-layouts: 42.6 us -> 3.74 us
  Pallas kernels: 0 us -> 35.7 us
  other arithmetic: 34.7 us -> 0 us
  waiting for transfers between devices: 23.7 us -> 0 us
    ppermute x28 -> x0, starting transfers between devices: 74.4 us -> none  [the longest x12 41.4 us: extended(): before = lax.ppermute(last, axis, up)]
    pallas_call x0 -> x1, Pallas kernels: none -> 35.7 us  [local(): pl.pallas_call(functools.partial(kernel, counts), out_shape=(jax.ShapeDty...]
    ppermute x28 -> x0, waiting for transfers between devices: 23.7 us -> none  [the longest x12 13.1 us: extended(): after = lax.ppermute(first, axis, down)]
    slice x20 -> x0, local copies, waits for them, and re-layouts: 16.6 us -> none  [the longest x14 11.4 us: extended(): last = lax.slice_in_dim(x, length - width, length, axis=dim)]
    concatenate x11 -> x0, other arithmetic: 11.3 us -> none  [extended(): x = jnp.concatenate([before, x, after], axis=dim)]
    ppermute x10 -> x0, local copies, waits for them, and re-layouts: 10.4 us -> none  [the longest x5 5.25 us: extended(): before = lax.ppermute(last, axis, up)]
    add x10 -> x0, other arithmetic: 9.24 us -> none  [the longest x8 7.78 us: jacobi(): neighbour + kappas[2] * field_pad[..., 1:-1, :-2]]
    another operation x15 -> x0, other arithmetic: 9.01 us -> none  [the longest x14 8.91 us: jacobi(): return jnp.stack([new_x, new_y])]
  transfers between devices with their start and end apart: 28 -> 0, of which waited for: 12 -> 0; matrix products, arithmetic and copies ran while one was open for 23% -> 0% of each run, Pallas kernels for 0% -> 0%
where the time goes in v2:
time: 40.2 us; the launch traced here: 40.1 us
  Pallas kernels  35.7 us (89%)
  local copies, waits for them, and re-layouts  3.74 us (9%)
  between operations  0.65 us (2%)
    pallas_call x1, Pallas kernels, local(): pl.pallas_call(functools.partial(kernel, counts), out_shape=(jax.ShapeDty...  35.7 us
    unnamed x6, local copies, waits for them, and re-layouts  3.74 us

profile of v2, /device:TPU:1, one launch (start us, length us, event | category | flops | bytes accessed | tf_op | source)
XLA Modules:
  0.0 40.1 jit_solution(7953857958752488449)
XLA Ops:
  0.6 0.0 copy-start
  0.6 0.9 %copy-done = f32[1,256,256]{2,1,0:T(8,128)S(1)} copy-done((f32[1,256,256]{2,1,0:T(8,128)S(1)}, f32[1,256,256]{2,1,0:T(8,128)}, u32[]{:S(2)}) %copy-start) | copy-done | bytes 262168
  1.6 0.0 copy-start.1
  1.6 0.9 %copy-done.1 = f32[1,256,256]{2,1,0:T(8,128)S(1)} copy-done((f32[1,256,256]{2,1,0:T(8,128)S(1)}, f32[1,256,256]{2,1,0:T(8,128)}, u32[]{:S(2)}) %copy-start.1) | copy-done | bytes 262168
  2.5 35.7 %shard_map.41 = (f32[5,1,256,256]{3,2,1,0:T(8,128)S(1)}, f32[2,1,256,256]{3,2,1,0:T(8,128)S(1)}) custom-call(f32[1,256,256]{2,1,0:T(8,128)S(1)} %copy-done, f32[1,256,256]{2,1,0:T(8,128)S(1)} %copy-done.1), custom_call_target="tpu_custom_call" | custom-call | tf_op jit(solution)/shard_map/pallas_call | solution.py:476
  38.2 1.1 %copy.6 = f32[5,1,256,256]{3,2,1,0:T(8,128)} copy(f32[5,1,256,256]{3,2,1,0:T(8,128)S(1)} %get-tuple-element.4) | data formatting | bytes 2621440
  39.3 0.8 %copy.7 = f32[2,1,256,256]{3,2,1,0:T(8,128)} copy(f32[2,1,256,256]{3,2,1,0:T(8,128)S(1)} %get-tuple-element.5) | data formatting | bytes 1048576
Async XLA Ops:
  0.6 1.0 %copy-start = (f32[1,256,256]{2,1,0:T(8,128)S(1)}, f32[1,256,256]{2,1,0:T(8,128)}, u32[]{:S(2)}) copy-start(f32[1,256,256]{2,1,0:T(8,128)} %images.1) | copy-start | bytes 786436
  1.6 0.9 %copy-start.1 = (f32[1,256,256]{2,1,0:T(8,128)S(1)}, f32[1,256,256]{2,1,0:T(8,128)}, u32[]{:S(2)}) copy-start(f32[1,256,256]{2,1,0:T(8,128)} %stiff.1) | copy-start | bytes 786436

commit v3 on v2

--- a/solution.py
+++ b/solution.py
@@ -17,13 +17,14 @@
 HALO = 16
 EDGE = HALO + 8
 SLOT = 16
+CHUNK = 96
 FOLD = LANES // (2 * SLOT)
 
 (
     TILE_B, ROW_A_UP, ROW_A_DOWN, ROW_S_UP, ROW_S_DOWN, FWD_TOP, FWD_BOTTOM, COL_RIGHT, COL_LEFT,
-    FWD_RIGHT, FWD_LEFT, FIELD_NEXT, FIELD_PREV, RIM_NEXT, RIM_PREV,
-) = range(15)
-KINDS = 15
+    FWD_RIGHT, FWD_LEFT,
+) = range(11)
+KINDS = 11
 
 
 def lane_roll(x, shift):
@@ -47,10 +48,10 @@
 
 def kernel(
     counts, images, stiff, tensor_out, field_out,
-    a, b, s, q, gx, gy, pr, p3, tt, ua, ub, uc, va, vb, vc, ex, ey, g0, g1, field,
+    a, b, s, q, gx, gy, pr, p3, tt, ua, ub, uc, va, vb, vc, ex, ey, g0, g1, field, last_field,
     send_right, send_left, got_left, got_right, next_left, next_right,
     rim, rim_before, rim_after, main_before, main_after,
-    local_sem, send_sem, recv_sem,
+    local_sem, send_sem, recv_sem, chunk_send, chunk_recv,
 ):
     sec, row, col = (lax.axis_index(name) for name in ("sec", "row", "col"))
     n_sec, n_row, n_col = counts
@@ -130,9 +131,12 @@
         clear(main_before)
 
     for start in (0, total - 8):
-        clear(a.at[:, pl.ds(start, 8)])
+        for ref in (a, q):
+            clear(ref.at[:, pl.ds(start, 8)])
+        for ref in (pr, p3, g0, g1):
+            clear(ref.at[:, :, pl.ds(start, 8)])
     for start in (8, total - 16):
-        for ref in (g0, g1, field):
+        for ref in (main_before, main_after):
             clear(ref.at[:, :, pl.ds(start, 8)])
 
     pl.semaphore_wait(barrier, sum(jnp.where(there, 1, 0) for there, _device in sides))
@@ -270,11 +274,29 @@
 
         return body
 
+    scale = jnp.where(has_next, jnp.float32(1.0), jnp.float32(0.0))
+    scale = scale * (1.0 / float((2 * RADIUS + 1) ** 2))
+
+    def window_mean(k, r, step):
+        lane = lanes_of(step)
+        summed = add(*(get(p3, r + d, step, k) for d in (-3, 0, 3)))
+        summed = add(summed, shifted(summed, 1, lane), shifted(summed, -1, lane))
+        summed = add(summed, shifted(summed, 3, lane), shifted(summed, -3, lane))
+        value = [x * scale for x in summed]
+        put(tt, value, r, step, k)
+        return value
+
     def three_first(r, step):
         for k in range(3):
             three_rows(k)(r, step)
 
     blocks(first, last, 16, three_first)
+
+    def mean_first(r, step):
+        for k in range(3):
+            window_mean(k, r, step)
+
+    blocks(first, last, 16, mean_first)
 
     when_got(has_next, tile_b + forward_rows + forward_cols)
     unpack(b, next_left, next_right, 0)
@@ -292,18 +314,10 @@
 
     blocks(first, last, 16, three_second)
 
-    scale = jnp.where(has_next, jnp.float32(1.0), jnp.float32(0.0))
-    scale = scale * (1.0 / float((2 * RADIUS + 1) ** 2))
-
     def tensor_block(r, step):
         lane = lanes_of(step)
-        parts = []
-        for k in range(5):
-            summed = add(*(get(p3, r + d, step, k) for d in (-3, 0, 3)))
-            summed = add(summed, shifted(summed, 1, lane), shifted(summed, -1, lane))
-            summed = add(summed, shifted(summed, 3, lane), shifted(summed, -3, lane))
-            parts.append([x * scale for x in summed])
-            put(tt, parts[-1], r, step, k)
+        parts = [get(tt, r, step, k) for k in range(3)]
+        parts += [window_mean(k, r, step) for k in (3, 4)]
         mid = get(q, r, step)
         around = add(
             get(q, r - 1, step), get(q, r + 1, step), shifted(mid, 1, lane), shifted(mid, -1, lane)
@@ -325,7 +339,77 @@
             g0[0, k, at, :] = x * mid[k]
             g0[1, k, at, :] = y * mid[k]
 
-    blocks(16, total - 16, 16, tensor_block)
+    def relaxed(source, r, step, x, y):
+        lane = lanes_of(step)
+
+        def near(part):
+            mid = get(source, r, step, part)
+            return add(
+                get(source, r - 1, step, part), get(source, r + 1, step, part),
+                shifted(mid, 1, lane), shifted(mid, -1, lane),
+            )
+
+        nx, ny = near(0), near(1)
+        ca, cb, cc = (get(ref, r, step) for ref in (ua, ub, uc))
+        return (
+            [x[k] + ca[k] * nx[k] - cb[k] * ny[k] for k in range(nb)],
+            [y[k] + cc[k] * ny[k] - cb[k] * nx[k] for k in range(nb)],
+        )
+
+    def sweep(source, target, scaled=None):
+        def body(r, step):
+            new = relaxed(source, r, step, get(ex, r, step), get(ey, r, step))
+            mid = get(q, r, step) if scaled is not None else None
+            for part in range(2):
+                if target is not None:
+                    put(target, new[part], r, step, part)
+                if scaled is not None:
+                    put(scaled, [m * x for m, x in zip(mid, new[part])], r, step, part)
+
+        return body
+
+    bounds = list(range(first, last - CHUNK + 1, CHUNK)) + [last]
+    chunks = len(bounds) - 1
+
+    def stages(c, bodies, lead):
+        for k, body in enumerate(bodies):
+            ahead = 8 * (lead - k)
+            low = first if c == 0 else bounds[c] + ahead
+            high = last if c == chunks - 1 else bounds[c + 1] + ahead
+            blocks(low, high, 24, body)
+
+    first_round = [tensor_block]
+    now, other = g0, g1
+    for k in range(1, SWEEPS):
+        first_round.append(sweep(now, field if k == SWEEPS - 1 else None, other))
+        now, other = other, now
+
+    to_next, to_prev = [], []
+    for c in range(chunks):
+        stages(c, first_round, SWEEPS - 1)
+        low, high = bounds[c], bounds[c + 1]
+        folded = pl.ds((low - first) // FOLD, (high - low) // FOLD)
+        pack_rim(field, rim, low, high, first, nw)
+        rows_sent = pl.ds(max(low, 16), min(high, total - 16) - max(low, 16))
+
+        def moves(rims, mains, device, way):
+            pairs = (
+                (rim.at[folded], rims.at[folded]),
+                (field.at[:, main, rows_sent], mains.at[:, main, rows_sent]),
+            )
+            return [
+                pltpu.make_async_remote_copy(
+                    src_ref=src, dst_ref=dst, send_sem=chunk_send.at[way + i, c],
+                    recv_sem=chunk_recv.at[way + i, c], device_id=device, device_id_type=MESH,
+                )
+                for i, (src, dst) in enumerate(pairs)
+            ]
+
+        to_next.append(moves(rim_before, main_before, next_id, 0))
+        to_prev.append(moves(rim_after, main_after, prev_id, 2))
+        when_start(has_next, to_next[c])
+        when_start(has_prev, to_prev[c])
+
     put_tensor = [
         pltpu.make_async_copy(
             tt.at[:, k, inner], tensor_out.at[:, 0, :, columns(k)], local_sem.at[0, k]
@@ -335,77 +419,13 @@
     for copy in put_tensor:
         copy.start()
 
-    def relaxed(source, r, step, x, y):
-        lane = lanes_of(step)
-
-        def near(part):
-            mid = get(source, r, step, part)
-            return add(
-                get(source, r - 1, step, part), get(source, r + 1, step, part),
-                shifted(mid, 1, lane), shifted(mid, -1, lane),
-            )
-
-        nx, ny = near(0), near(1)
-        ca, cb, cc = (get(ref, r, step) for ref in (ua, ub, uc))
-        return (
-            [x[k] + ca[k] * nx[k] - cb[k] * ny[k] for k in range(nb)],
-            [y[k] + cc[k] * ny[k] - cb[k] * nx[k] for k in range(nb)],
-        )
-
-    def sweep(source, target, final, low, high):
-        def body(r, step):
-            new = relaxed(source, r, step, get(ex, r, step), get(ey, r, step))
-            if not final:
-                mid = get(q, r, step)
-                new = [[m * x for m, x in zip(mid, part)] for part in new]
-            for part in range(2):
-                put(target, new[part], r, step, part)
-
-        blocks(low, high, 32, body)
-
-    now, other = g0, g1
-    for k in range(1, SWEEPS):
-        final = k == SWEEPS - 1
-        sweep(now, field if final else other, final, 16, total - 16)
-        if not final:
-            now, other = other, now
-
-    span = pl.ds(16, total - 32)
-    rim[...] = packed_rim(field, piece, first, nw, lane)
-    to_next = [
-        remote(rim, rim_before, RIM_NEXT, next_id),
-        remote(field.at[:, main, span], main_before, FIELD_NEXT, next_id),
-    ]
-    to_prev = [
-        remote(rim, rim_after, RIM_PREV, prev_id),
-        remote(field.at[:, main, span], main_after, FIELD_PREV, prev_id),
-    ]
-    when_start(has_next, to_next)
-    when_start(has_prev, to_prev)
-    def scale_block(r, step):
-        mid = get(q, r, step)
-        for part in range(2):
-            put(g0, [m * x for m, x in zip(mid, get(field, r, step, part))], r, step, part)
-
-    blocks(16, total - 16, 32, scale_block)
-    when_got(has_prev, to_next)
-    when_got(has_next, to_prev)
-
-    both = rim_before[...] + rim_after[...]
-    for j in range(FOLD):
-        for k, ref in enumerate((gx, gy)):
-            low = (2 * j + k) * SLOT
-            head = jnp.where(lane < 8, lane_roll(both, -low), 0.0)
-            tail = lane_roll(both, LANES - 16 - low)
-            ref[nw, pl.ds(first + j * piece, piece), :] = jnp.where(lane >= LANES - 8, tail, head)
 
     def first_block(r, step):
-        there = pl.ds(r - 16, step)
         at = pl.ds(r, step)
 
         def beside(part, ref):
             return [
-                main_before[part, k, there, :] + main_after[part, k, there, :] for k in range(nw)
+                main_before[part, k, at, :] + main_after[part, k, at, :] for k in range(nw)
             ] + [ref[nw, at, :]]
 
         x, y = beside(0, gx), beside(1, gy)
@@ -416,24 +436,43 @@
         put(ex, new_x, r, step)
         put(ey, new_y, r, step)
         mid = get(q, r, step)
-        for part, values in enumerate(relaxed(g0, r, step, new_x, new_y)):
-            put(g1, [m * v for m, v in zip(mid, values)], r, step, part)
-
-    blocks(16, total - 16, 16, first_block)
-    when_sent(has_next, to_next)
-    when_sent(has_prev, to_prev)
-    now, other = g1, g0
+        for part, values in enumerate(relaxed(now, r, step, new_x, new_y)):
+            put(other, [m * v for m, v in zip(mid, values)], r, step, part)
+
+    second_round = [first_block]
+    source, target = other, now
     for k in range(1, SWEEPS):
-        final = k == SWEEPS - 1
-        if final:
-            sweep(now, field, final, EDGE, end)
+        if k == SWEEPS - 1:
+            second_round.append(sweep(source, last_field))
         else:
-            sweep(now, other, final, 16, total - 16)
-        now, other = other, now
+            second_round.append(sweep(source, None, target))
+        source, target = target, source
+
+    for c in range(chunks):
+        when_got(has_prev, to_next[c])
+        when_got(has_next, to_prev[c])
+        low, high = bounds[c], bounds[c + 1]
+        size = (high - low) // FOLD
+        folded = pl.ds((low - first) // FOLD, size)
+        both = rim_before[folded, :] + rim_after[folded, :]
+        lane = lanes_of(size)
+        for j in range(FOLD):
+            for k, ref in enumerate((gx, gy)):
+                slot = (2 * j + k) * SLOT
+                head = jnp.where(lane < 8, lane_roll(both, -slot), 0.0)
+                tail = lane_roll(both, LANES - 16 - slot)
+                ref[nw, pl.ds(low + j * size, size), :] = jnp.where(
+                    lane >= LANES - 8, tail, head
+                )
+        stages(c, second_round, 0)
+
+    for c in range(chunks):
+        when_sent(has_next, to_next[c])
+        when_sent(has_prev, to_prev[c])
 
     put_field = [
         pltpu.make_async_copy(
-            field.at[:, k, inner], field_out.at[:, 0, :, columns(k)], local_sem.at[1, k]
+            last_field.at[:, k, inner], field_out.at[:, 0, :, columns(k)], local_sem.at[1, k]
         )
         for k in range(nw)
     ]
@@ -448,18 +487,19 @@
         copy.wait()
 
 
-def packed_rim(field, piece, first, nw, lane):
-    out = jnp.zeros((piece, LANES), jnp.float32)
+def pack_rim(field, rim, low, high, first, nw):
+    size = (high - low) // FOLD
+    lane = lax.broadcasted_iota(jnp.int32, (size, LANES), 1)
+    out = jnp.zeros((size, LANES), jnp.float32)
     for j in range(FOLD):
-        at = pl.ds(first + j * piece, piece)
+        at = pl.ds(low + j * size, size)
         for k in range(2):
-            low = (2 * j + k) * SLOT
+            slot = (2 * j + k) * SLOT
             block = field[k, nw, at, :]
-            head = lane_roll(block, low)
-            tail = lane_roll(block, low + SLOT)
-            out = jnp.where((lane >= low) & (lane < low + 8), head, out)
-            out = jnp.where((lane >= low + 8) & (lane < low + 16), tail, out)
-    return out
+            head, tail = lane_roll(block, slot), lane_roll(block, slot + SLOT)
+            out = jnp.where((lane >= slot) & (lane < slot + 8), head, out)
+            out = jnp.where((lane >= slot + 8) & (lane < slot + 16), tail, out)
+    rim[pl.ds((low - first) // FOLD, size), :] = out
 
 
 def local(counts, images, stiffness):
@@ -472,7 +512,8 @@
     five = pltpu.VMEM((5, nb, total, LANES), f32)
     pair = pltpu.VMEM((2, nb, total, LANES), f32)
     packet = pltpu.VMEM(((total - 16) // FOLD, LANES), f32)
-    mains = pltpu.VMEM((2, nw, total - 32, LANES), f32)
+    mains = pltpu.VMEM((2, nw, total, LANES), f32)
+    chunks = (total - 16) // CHUNK
     return pl.pallas_call(
         functools.partial(kernel, counts),
         out_shape=(
@@ -484,13 +525,15 @@
         scratch_shapes=[plane] * 6
         + [five] * 3
         + [plane] * 8
-        + [pair] * 3
+        + [pair] * 4
         + [packet] * 9
         + [mains] * 2
         + [
             pltpu.SemaphoreType.DMA((2, nw)),
             pltpu.SemaphoreType.DMA((KINDS, nw)),
             pltpu.SemaphoreType.DMA((KINDS, nw)),
+            pltpu.SemaphoreType.DMA((4, chunks)),
+            pltpu.SemaphoreType.DMA((4, chunks)),
         ],
         compiler_params=pltpu.CompilerParams(
             collective_id=0, has_side_effects=True, vmem_limit_bytes=48 * 1024 * 1024

time: 40.2 us -> 35.7 us (0.89)
  Pallas kernels: 35.7 us -> 31.2 us
    pallas_call x1, Pallas kernels: 35.7 us -> 31.2 us  [local(): pl.pallas_call(functools.partial(kernel, counts), out_shape=(jax.ShapeDty...]
where the time goes in v3:
time: 35.7 us; the launch traced here: 35.6 us
  Pallas kernels  31.2 us (87%)
  local copies, waits for them, and re-layouts  3.74 us (10%)
  between operations  0.65 us (2%)
    pallas_call x1, Pallas kernels, local(): pl.pallas_call(functools.partial(kernel, counts), out_shape=(jax.ShapeDty...  31.2 us
    unnamed x6, local copies, waits for them, and re-layouts  3.74 us

profile of v3, /device:TPU:1, one launch (start us, length us, event | category | flops | bytes accessed | tf_op | source)
XLA Modules:
  0.0 35.6 jit_solution(13572268839853732729)
XLA Ops:
  0.6 0.0 copy-start
  0.6 0.9 %copy-done = f32[1,256,256]{2,1,0:T(8,128)S(1)} copy-done((f32[1,256,256]{2,1,0:T(8,128)S(1)}, f32[1,256,256]{2,1,0:T(8,128)}, u32[]{:S(2)}) %copy-start) | copy-done | bytes 262168
  1.6 0.0 copy-start.1
  1.6 0.9 %copy-done.1 = f32[1,256,256]{2,1,0:T(8,128)S(1)} copy-done((f32[1,256,256]{2,1,0:T(8,128)S(1)}, f32[1,256,256]{2,1,0:T(8,128)}, u32[]{:S(2)}) %copy-start.1) | copy-done | bytes 262168
  2.5 31.2 %shard_map.41 = (f32[5,1,256,256]{3,2,1,0:T(8,128)S(1)}, f32[2,1,256,256]{3,2,1,0:T(8,128)S(1)}) custom-call(f32[1,256,256]{2,1,0:T(8,128)S(1)} %copy-done, f32[1,256,256]{2,1,0:T(8,128)S(1)} %copy-done.1), custom_call_target="tpu_custom_call" | custom-call | tf_op jit(solution)/shard_map/pallas_call | solution.py:517
  33.7 1.1 %copy.6 = f32[5,1,256,256]{3,2,1,0:T(8,128)} copy(f32[5,1,256,256]{3,2,1,0:T(8,128)S(1)} %get-tuple-element.4) | data formatting | bytes 2621440
  34.8 0.8 %copy.7 = f32[2,1,256,256]{3,2,1,0:T(8,128)} copy(f32[2,1,256,256]{3,2,1,0:T(8,128)S(1)} %get-tuple-element.5) | data formatting | bytes 1048576
Async XLA Ops:
  0.6 1.0 %copy-start = (f32[1,256,256]{2,1,0:T(8,128)S(1)}, f32[1,256,256]{2,1,0:T(8,128)}, u32[]{:S(2)}) copy-start(f32[1,256,256]{2,1,0:T(8,128)} %images.1) | copy-start | bytes 786436
  1.6 0.9 %copy-start.1 = (f32[1,256,256]{2,1,0:T(8,128)S(1)}, f32[1,256,256]{2,1,0:T(8,128)}, u32[]{:S(2)}) copy-start(f32[1,256,256]{2,1,0:T(8,128)} %stiff.1) | copy-start | bytes 786436

commit v4 on v3

--- a/solution.py
+++ b/solution.py
@@ -133,10 +133,10 @@
     for start in (0, total - 8):
         for ref in (a, q):
             clear(ref.at[:, pl.ds(start, 8)])
-        for ref in (pr, p3, g0, g1):
+        for ref in (pr, p3):
             clear(ref.at[:, :, pl.ds(start, 8)])
     for start in (8, total - 16):
-        for ref in (main_before, main_after):
+        for ref in (g0, g1, field):
             clear(ref.at[:, :, pl.ds(start, 8)])
 
     pl.semaphore_wait(barrier, sum(jnp.where(there, 1, 0) for there, _device in sides))
@@ -296,7 +296,7 @@
         for k in range(3):
             window_mean(k, r, step)
 
-    blocks(first, last, 16, mean_first)
+    blocks(16, total - 16, 16, mean_first)
 
     when_got(has_next, tile_b + forward_rows + forward_cols)
     unpack(b, next_left, next_right, 0)
@@ -371,11 +371,12 @@
     bounds = list(range(first, last - CHUNK + 1, CHUNK)) + [last]
     chunks = len(bounds) - 1
 
-    def stages(c, bodies, lead):
+    def stages(c, bodies, lead, ends):
         for k, body in enumerate(bodies):
             ahead = 8 * (lead - k)
-            low = first if c == 0 else bounds[c] + ahead
-            high = last if c == chunks - 1 else bounds[c + 1] + ahead
+            margin = ends[k == len(bodies) - 1]
+            low = first + margin if c == 0 else bounds[c] + ahead
+            high = last - margin if c == chunks - 1 else bounds[c + 1] + ahead
             blocks(low, high, 24, body)
 
     first_round = [tensor_block]
@@ -386,7 +387,7 @@
 
     to_next, to_prev = [], []
     for c in range(chunks):
-        stages(c, first_round, SWEEPS - 1)
+        stages(c, first_round, SWEEPS - 1, (8, 8))
         low, high = bounds[c], bounds[c + 1]
         folded = pl.ds((low - first) // FOLD, (high - low) // FOLD)
         pack_rim(field, rim, low, high, first, nw)
@@ -464,7 +465,7 @@
                 ref[nw, pl.ds(low + j * size, size), :] = jnp.where(
                     lane >= LANES - 8, tail, head
                 )
-        stages(c, second_round, 0)
+        stages(c, second_round, 0, (8, 16))
 
     for c in range(chunks):
         when_sent(has_next, to_next[c])
@@ -536,7 +537,7 @@
             pltpu.SemaphoreType.DMA((4, chunks)),
         ],
         compiler_params=pltpu.CompilerParams(
-            collective_id=0, has_side_effects=True, vmem_limit_bytes=48 * 1024 * 1024
+            collective_id=0, has_side_effects=True, vmem_limit_bytes=67043328
         ),
     )(images, stiffness)
 

time: 35.7 us -> 35.7 us (level)
  Pallas kernels: 31.2 us -> 31.6 us
  local copies, waits for them, and re-layouts: 3.74 us -> 3.36 us
    pallas_call x1, Pallas kernels: 31.2 us -> 31.6 us  [local(): pl.pallas_call(functools.partial(kernel, counts), out_shape=(jax.ShapeDty...]
    unnamed x6 -> x4, local copies, waits for them, and re-layouts: 3.74 us -> 3.36 us
where the time goes in v4:
time: 35.7 us; the launch traced here: 35.6 us
  Pallas kernels  31.6 us (89%)
  local copies, waits for them, and re-layouts  3.36 us (9%)
  between operations  0.65 us (2%)
    pallas_call x1, Pallas kernels, local(): pl.pallas_call(functools.partial(kernel, counts), out_shape=(jax.ShapeDty...  31.6 us
    unnamed x4, local copies, waits for them, and re-layouts  3.36 us

profile of v4, /device:TPU:1, one launch (start us, length us, event | category | flops | bytes accessed | tf_op | source)
XLA Modules:
  0.0 35.6 jit_solution(1131921239120896643)
XLA Ops:
  0.6 31.6 %shard_map.41 = (f32[5,1,256,256]{3,2,1,0:T(8,128)}, f32[2,1,256,256]{3,2,1,0:T(8,128)}) custom-call(f32[1,256,256]{2,1,0:T(8,128)} %images.1, f32[1,256,256]{2,1,0:T(8,128)} %stiff.1), custom_call_target="tpu_custom_call" | custom-call | tf_op jit(solution)/shard_map/pallas_call | solution.py:518
  32.2 0.0 copy-start
  32.2 2.6 %copy.6 = f32[5,1,256,256]{3,2,1,0:T(8,128)} copy(f32[5,1,256,256]{3,2,1,0:T(8,128)} %get-tuple-element.4) | data formatting | bytes 2621440
  34.8 0.0 copy-done
  34.8 0.8 %copy.7 = f32[2,1,256,256]{3,2,1,0:T(8,128)} copy(f32[2,1,256,256]{3,2,1,0:T(8,128)S(1)} %copy-done) | data formatting | bytes 1048576
Async XLA Ops:
  32.2 2.6 %copy-start = (f32[2,1,256,256]{3,2,1,0:T(8,128)S(1)}, f32[2,1,256,256]{3,2,1,0:T(8,128)}, u32[]{:S(2)}) copy-start(f32[2,1,256,256]{3,2,1,0:T(8,128)} %get-tuple-element.5) | copy-start | bytes 1572868

commit v5 on v4

--- a/solution.py
+++ b/solution.py
@@ -537,9 +537,9 @@
             pltpu.SemaphoreType.DMA((4, chunks)),
         ],
         compiler_params=pltpu.CompilerParams(
-            collective_id=0, has_side_effects=True, vmem_limit_bytes=67043328
+            collective_id=0, has_side_effects=True, vmem_limit_bytes=48 * 1024 * 1024
         ),
-    )(images, stiffness)
+    )(*(pltpu.with_memory_space_constraint(x, pltpu.HBM) for x in (images, stiffness)))
 
 
 def solution(mesh):

time: 35.7 us -> 33.4 us (0.936)
  local copies, waits for them, and re-layouts: 3.36 us -> 1.85 us
  Pallas kernels: 31.6 us -> 30.8 us
    unnamed x4 -> x2, local copies, waits for them, and re-layouts: 3.36 us -> 1.85 us
    pallas_call x1, Pallas kernels: 31.6 us -> 30.8 us  [local(): pl.pallas_call(functools.partial(kernel, counts), out_shape=(jax.ShapeDty...]
where the time goes in v5:
time: 33.4 us; the launch traced here: 33.3 us
  Pallas kernels  30.8 us (92%)
  local copies, waits for them, and re-layouts  1.85 us (6%)
  between operations  0.64 us (2%)
    pallas_call x1, Pallas kernels, local(): pl.pallas_call(functools.partial(kernel, counts), out_shape=(jax.ShapeDty...  30.8 us
    unnamed x2, local copies, waits for them, and re-layouts  1.85 us

profile of v5, /device:TPU:1, one launch (start us, length us, event | category | flops | bytes accessed | tf_op | source)
XLA Modules:
  0.0 33.3 jit_solution(18378091845190797153)
XLA Ops:
  0.6 30.8 %shard_map.41 = (f32[5,1,256,256]{3,2,1,0:T(8,128)S(1)}, f32[2,1,256,256]{3,2,1,0:T(8,128)S(1)}) custom-call(f32[1,256,256]{2,1,0:T(8,128)} %images.1, f32[1,256,256]{2,1,0:T(8,128)} %stiff.1), custom_call_target="tpu_custom_call" | custom-call | tf_op jit(solution)/shard_map/pallas_call | solution.py:518
  31.4 1.1 %copy.6 = f32[5,1,256,256]{3,2,1,0:T(8,128)} copy(f32[5,1,256,256]{3,2,1,0:T(8,128)S(1)} %get-tuple-element.4) | data formatting | bytes 2621440
  32.5 0.8 %copy.7 = f32[2,1,256,256]{3,2,1,0:T(8,128)} copy(f32[2,1,256,256]{3,2,1,0:T(8,128)S(1)} %get-tuple-element.5) | data formatting | bytes 1048576

commit v6 on v5

--- a/solution.py
+++ b/solution.py
@@ -17,7 +17,7 @@
 HALO = 16
 EDGE = HALO + 8
 SLOT = 16
-CHUNK = 96
+CHUNK = 64
 FOLD = LANES // (2 * SLOT)
 
 (
@@ -377,7 +377,7 @@
             margin = ends[k == len(bodies) - 1]
             low = first + margin if c == 0 else bounds[c] + ahead
             high = last - margin if c == chunks - 1 else bounds[c + 1] + ahead
-            blocks(low, high, 24, body)
+            blocks(low, high, 32, body)
 
     first_round = [tensor_block]
     now, other = g0, g1

time: 33.4 us -> 32.2 us (0.964)
  Pallas kernels: 30.8 us -> 29.5 us
    pallas_call x1, Pallas kernels: 30.8 us -> 29.5 us  [local(): pl.pallas_call(functools.partial(kernel, counts), out_shape=(jax.ShapeDty...]
where the time goes in v6:
time: 32.2 us; the launch traced here: 32 us
  Pallas kernels  29.5 us (92%)
  local copies, waits for them, and re-layouts  1.85 us (6%)
  between operations  0.64 us (2%)
    pallas_call x1, Pallas kernels, local(): pl.pallas_call(functools.partial(kernel, counts), out_shape=(jax.ShapeDty...  29.5 us
    unnamed x2, local copies, waits for them, and re-layouts  1.85 us

profile of v6, /device:TPU:1, one launch (start us, length us, event | category | flops | bytes accessed | tf_op | source)
XLA Modules:
  0.0 32.0 jit_solution(11956204164261322845)
XLA Ops:
  0.6 29.5 %shard_map.41 = (f32[5,1,256,256]{3,2,1,0:T(8,128)S(1)}, f32[2,1,256,256]{3,2,1,0:T(8,128)S(1)}) custom-call(f32[1,256,256]{2,1,0:T(8,128)} %images.1, f32[1,256,256]{2,1,0:T(8,128)} %stiff.1), custom_call_target="tpu_custom_call" | custom-call | tf_op jit(solution)/shard_map/pallas_call | solution.py:518
  30.2 1.1 %copy.6 = f32[5,1,256,256]{3,2,1,0:T(8,128)} copy(f32[5,1,256,256]{3,2,1,0:T(8,128)S(1)} %get-tuple-element.4) | data formatting | bytes 2621440
  31.2 0.8 %copy.7 = f32[2,1,256,256]{3,2,1,0:T(8,128)} copy(f32[2,1,256,256]{3,2,1,0:T(8,128)S(1)} %get-tuple-element.5) | data formatting | bytes 1048576
